TPU v7x, 32 devices: a whole 2x2x4 slice. The times are simulated.
32 devices in a mesh: gossip: 8 (over z, x), fsdp: 4 (over y, core).
Axes of the slice: x: 2, y: 2, z: 4, core: 2. Of those that a mesh axis runs over, the one named last changes fastest.
Arguments:
- series: bfloat16 [8, 2, 512, 768], P('gossip', None, 'fsdp'), may hold values from -6 to 6
- cotangent: bfloat16 [8, 2, 512, 768], P('gossip', None, 'fsdp'), may hold values from -6 to 6
- observed: int32 [8, 2, 512], P('gossip', None, 'fsdp'), may hold values 0 or 1
- depth_kernel: float32 [7, 768], replicated, may hold values from -2.5 to 2.5
- norm_gain: float32 [768], replicated, may hold values from 0.1 to 1.9
- layer_scale: float32 [768], replicated, may hold values from 0.5 to 2
- step_index: int32 [1], replicated, may hold values from 0 to 999
- w_expand: bfloat16 [8, 768, 4096], P('gossip', 'fsdp'), may hold values from -4 to 4
- w_project: bfloat16 [8, 4096, 768], P('gossip', 'fsdp'), may hold values from -4 to 4
- first_expand: float32 [8, 768, 4096], P('gossip', 'fsdp'), may hold values from -3 to 3
- second_expand: float32 [8, 768, 4096], P('gossip', 'fsdp'), may hold values from 0.1 to 2
- first_project: float32 [8, 4096, 768], P('gossip', 'fsdp'), may hold values from -3 to 3
- second_project: float32 [8, 4096, 768], P('gossip', 'fsdp'), may hold values from 0.1 to 2
Outputs:
- shared_expand: bfloat16 [8, 768, 4096], P('gossip', 'fsdp')
- shared_project: bfloat16 [8, 4096, 768], P('gossip', 'fsdp')
- first_expand_next: float32 [8, 768, 4096], P('gossip', 'fsdp')
- second_expand_next: float32 [8, 768, 4096], P('gossip', 'fsdp')
- first_project_next: float32 [8, 4096, 768], P('gossip', 'fsdp')
- second_project_next: float32 [8, 4096, 768], P('gossip', 'fsdp')
- input_grad: bfloat16 [8, 2, 512, 768], P('gossip', None, 'fsdp')
All inputs are finite; a program needn't handle non-finite values. No bound on the sum of `observed` on one device may be relied on, other than what follows from the above.
Results may differ from a plain program's by a relative error of at most 0.0095.
Values may be sent and summed in bfloat16 or wider, within the bound.
No kernel may reach another device: no remote copies, remote signals or barrier semaphores. Data moves between devices by JAX's collectives and lax.ppermute only.
A program may use at most 128 MiB of HBM per device.

v0:
```python
from functools import partial
import math

import jax
import jax.numpy as jnp
from jax import lax
from jax.experimental import pallas as pl
from jax.experimental.pallas import tpu as pltpu
from jax.sharding import PartitionSpec as P

NORM_EPS = 1e-06
ADAM_EPS = 1e-08
BETA_ONE = 0.9
BETA_TWO = 0.999
LEARN_RATE = 0.02
DECAY_RATE = 0.1
HALF_ROOT = 0.7071067811865476
INV_ROOT_TAU = 0.3989422804014327
PAD = 8
BLOCK = 256
F32 = jnp.float32
BF16 = jnp.bfloat16
MIB = 1 << 20


def dims(lhs, rhs):
    return (((lhs,), (rhs,)), ((), ()))


def dot(lhs, rhs, contract=(1, 0)):
    return lax.dot_general(lhs, rhs, dims(*contract), preferred_element_type=F32)


def whole(array):
    rank = len(array.shape)
    return pl.BlockSpec(array.shape, lambda *ids: (0,) * rank)


def hbm():
    return pl.BlockSpec(memory_space=pl.ANY)


def params(limit):
    return pltpu.CompilerParams(vmem_limit_bytes=limit)


def cost(moved=1):
    return pl.CostEstimate(flops=1, transcendentals=0, bytes_accessed=moved)


def loop(count, body, unroll=False):
    if count > 4 or not unroll:
        lax.fori_loop(0, count, lambda i, carry: (body(i), carry)[1], 0)
    else:
        for i in range(count):
            body(i)


def row_range(i, rows):
    return pl.ds(i * rows if isinstance(i, int) else pl.multiple_of(i * rows, rows), rows)


def ranges(sizes):
    starts = [sum(sizes[:i]) for i in range(len(sizes))]
    return list(zip(starts, sizes))


def plan(owned):
    if owned % 1024 == 0:
        q = owned // 4
        return ranges([2 * q, 2 * q]), ranges([q] * 4), ranges([2 * q, 2 * q])
    half = owned // 2
    return ranges([owned]), ranges([half, half]), ranges([owned])


def xor_perm(value, off):
    count = lax.axis_size("fsdp")
    return lax.ppermute(value, "fsdp", [(i, i ^ off) for i in range(count)])


def gather_xor(own, hold=()):
    count = lax.axis_size("fsdp")
    pieces = {0: own}
    bit = count // 2
    while bit:
        for off in list(pieces):
            value = pieces[off]
            if off and len(hold):
                value = lax.optimization_barrier((value, *hold))[0]
            pieces[off ^ bit] = xor_perm(value, bit)
        bit //= 2
    return [pieces[off] for off in range(count)]


def send_packs(packs):
    return [xor_perm(pack, 2 * h) if h else pack for h, pack in enumerate(packs)]


def relay_packs(packs, hold=()):
    held = []
    for h, pack in enumerate(packs):
        out = lax.optimization_barrier((pack, *hold))[0] if h and len(hold) else pack
        held += [pack, xor_perm(out, 1)]
    return held


def pieces_of(held, base, spans, k):
    return [(array, base + off % 2 * spans + k) for off, array in enumerate(held)]


def swap_blocks(blocks):
    return [block if off == 0 else xor_perm(block, off) for off, block in enumerate(blocks)]


def swap_gossip(value, level):
    count = lax.axis_size("gossip")
    return lax.ppermute(value, "gossip", [(i, i ^ (1 << level)) for i in range(count)])


def token_kernel(*refs):
    refs[-1][...] = jnp.zeros(refs[-1].shape, F32)


def token(value, name):
    shape = jax.ShapeDtypeStruct((8, 128), F32)
    return pl.pallas_call(
        token_kernel,
        out_shape=shape,
        in_specs=[hbm()],
        out_specs=pl.BlockSpec(memory_space=pltpu.VMEM),
        compiler_params=params(MIB),
        cost_estimate=cost(40 * MIB),
        name=name,
    )(value)


def slice_kernel(me_ref, *refs, count):
    outs = refs[-(count // 2) :]
    rows = refs[0].shape[0]
    for off in range(count):
        low = off % 2 * rows
        outs[off // 2][low : low + rows] = refs[off][...]


def slice_specs(rows, full, count, span):
    start, size = span
    ratio = full // count // size
    base = start // size
    return [
        pl.BlockSpec((rows, size), lambda i, me, off=off: (0, (me[0] ^ off) * ratio + base))
        for off in range(count)
    ]


def slice_weights(me, w, count, span):
    rows, full = w.shape
    shape = jax.ShapeDtypeStruct((2 * rows, span[1]), w.dtype)
    return pl.pallas_call(
        partial(slice_kernel, count=count),
        out_shape=[shape] * (count // 2),
        grid_spec=pltpu.PrefetchScalarGridSpec(
            num_scalar_prefetch=1,
            grid=(1,),
            in_specs=slice_specs(rows, full, count, span),
            out_specs=[whole(shape)] * (count // 2),
        ),
        compiler_params=params(16 * MIB),
        cost_estimate=cost(),
        name=f"slice_{span[0]}",
    )(me, *[w] * count)


def pack_kernel(me_ref, cot_ref, seen_ref, scale_ref, *refs, count):
    *outs, masked_ref = refs[-(count // 2) - 1 :]
    blocks = refs[: -(count // 2) - 1]
    spans = len(blocks) // count
    rows, width = cot_ref.shape
    part, size = blocks[0].shape
    panels = width // size
    masked = (cot_ref[...].astype(F32) * seen_ref[...]).astype(BF16)
    masked_ref[...] = masked
    branch = (masked.astype(F32) * scale_ref[...]).astype(BF16)
    for out in outs:
        for p in range(panels):
            out[p * rows : (p + 1) * rows] = branch[:, p * size : (p + 1) * size]
    for off in range(count):
        for k in range(spans):
            low = panels * rows + (off % 2 * spans + k) * part
            outs[off // 2][low : low + part] = blocks[k * count + off][...]


def pack_first(me, cot, seen, scale, w, count, spans):
    rows, width = cot.shape
    part, full = w.shape
    size = spans[0][1]
    shape = jax.ShapeDtypeStruct((width // size * rows + 2 * len(spans) * part, size), BF16)
    *packs, masked = pl.pallas_call(
        partial(pack_kernel, count=count),
        out_shape=[shape] * (count // 2) + [jax.ShapeDtypeStruct(cot.shape, BF16)],
        grid_spec=pltpu.PrefetchScalarGridSpec(
            num_scalar_prefetch=1,
            grid=(1,),
            in_specs=[whole(cot), whole(seen), whole(scale)]
            + [spec for span in spans for spec in slice_specs(part, full, count, span)],
            out_specs=[whole(shape)] * (count // 2) + [whole(cot)],
        ),
        compiler_params=params(24 * MIB),
        cost_estimate=cost(),
        name="pack_first",
    )(me, cot, seen, scale, *[w] * (count * len(spans)))
    return packs, masked


def norm_kernel(me_ref, taps_ref, gain_ref, *refs, count, tile):
    pieces = refs[:count]
    normed_ref, turned_ref, unit_ref, inv_ref, padded = refs[-5:]
    off = pl.program_id(0)
    seqs, steps, width = pieces[0].shape
    taps = taps_ref.shape[0]
    reach = taps // 2
    me = me_ref[0]

    @pl.when(off == 0)
    def _():
        edge = jnp.zeros((seqs, PAD, width), F32)
        padded[:, :PAD] = edge
        padded[:, PAD + count * steps :] = edge
        for other in range(count):
            start = pl.multiple_of((me ^ other) * steps + PAD, 8)
            padded[:, pl.ds(start, steps)] = pieces[other][...].astype(F32)

    def body(i, carry):
        s = i // (steps // tile)
        r = i % (steps // tile)
        base = pl.multiple_of((me ^ off) * steps + r * tile, 8)
        window = padded.at[s, pl.ds(base, tile + 2 * PAD)]
        conv = jnp.zeros((tile, width), F32)
        for j in range(taps):
            low = PAD + j - reach
            conv = conv + taps_ref[j : j + 1] * window[low : low + tile]
        centred = conv - jnp.mean(conv, axis=-1, keepdims=True)
        inv = lax.rsqrt(jnp.mean(centred * centred, axis=-1, keepdims=True) + NORM_EPS)
        unit = centred * inv
        rows = pl.ds(pl.multiple_of(i * tile, tile), tile)
        normed_ref[rows] = (unit * gain_ref[...]).astype(BF16)

        @pl.when(off == 0)
        def _():
            unit_ref[rows] = unit
            inv_ref[rows] = jnp.broadcast_to(inv, (tile, 128))

        return carry

    lax.fori_loop(0, seqs * steps // tile, body, 0)
    turned_ref[...] = normed_ref[...].T


def norm_rows(me, pieces, taps, gain, after):
    count = len(pieces)
    seqs, steps, width = pieces[0].shape
    rows = seqs * steps
    total = count * rows
    return pl.pallas_call(
        partial(norm_kernel, count=count, tile=math.gcd(steps, 128)),
        out_shape=[
            jax.ShapeDtypeStruct((total, width), BF16),
            jax.ShapeDtypeStruct((width, total), BF16),
            jax.ShapeDtypeStruct((rows, width), F32),
            jax.ShapeDtypeStruct((rows, 128), F32),
        ],
        grid_spec=pltpu.PrefetchScalarGridSpec(
            num_scalar_prefetch=1,
            grid=(count,),
            in_specs=[whole(taps), whole(gain)]
            + [whole(p) for p in pieces]
            + [hbm()] * len(after),
            out_specs=[
                pl.BlockSpec((rows, width), lambda i, m: (i, 0)),
                pl.BlockSpec((width, rows), lambda i, m: (0, i)),
                pl.BlockSpec((rows, width), lambda i, m: (0, 0)),
                pl.BlockSpec((rows, 128), lambda i, m: (0, 0)),
            ],
            scratch_shapes=[pltpu.VMEM((seqs, count * steps + 2 * PAD, width), F32)],
        ),
        compiler_params=params(18 * MIB + 14 * total * width // 2),
        cost_estimate=cost(40 * MIB),
        name="norm_rows",
    )(me, taps, gain, *pieces, *after)


def adam(weight, first, second, gradient, inv_one, inv_two):
    first_next = BETA_ONE * first + (1.0 - BETA_ONE) * gradient
    second_next = BETA_TWO * second + (1.0 - BETA_TWO) * gradient * gradient
    weight_f = weight.astype(F32)
    direction = first_next * inv_one / (jnp.sqrt(second_next * inv_two) + ADAM_EPS)
    updated = (weight_f - LEARN_RATE * (direction + DECAY_RATE * weight_f)).astype(BF16)
    return updated, first_next, second_next


def adam_tiles(w_ref, m_ref, v_ref, gradient, corr_ref, updated_ref, first_ref, second_ref, tile):
    def body(i, carry):
        rows = pl.ds(pl.multiple_of(i * tile, tile), tile)
        updated, first, second = adam(
            w_ref[rows], m_ref[rows], v_ref[rows], gradient(rows), corr_ref[0], corr_ref[1]
        )
        updated_ref[rows] = updated
        first_ref[rows] = first
        second_ref[rows] = second
        return carry

    lax.fori_loop(0, w_ref.shape[0] // tile, body, 0)


def join_rows(me, pieces, joined, columns=slice(None)):
    part = pieces[0].shape[0]
    for off, piece in enumerate(pieces):
        start = pl.multiple_of((me ^ off) * part, 16)
        joined[pl.ds(start, part), columns] = piece[...]


def hidden_kernel(me_ref, corr_ref, normed_ref, w_ref, m_ref, v_ref, *refs, count, first):
    wide = refs[:count]
    if first:
        packs = refs[count : 2 * count]
        updated_ref, first_ref, second_ref, slope_ref, grads_ref, joined, total = refs[-7:]
    else:
        grads_ref = refs[count]
        updated_ref, first_ref, second_ref, slope_ref, joined, total = refs[-6:]
    join_rows(me_ref[0], wide, joined)
    width = normed_ref.shape[1]
    rows = normed_ref.shape[0] // count
    scale_in = 1.0 / math.sqrt(width)
    if first:
        size = packs[0].shape[1]
        for off in range(count):
            for p in range(width // size):
                grads_ref[off * rows : (off + 1) * rows, p * size : (p + 1) * size] = packs[off][
                    p * rows : (p + 1) * rows
                ]
    total[...] = jnp.zeros(total.shape, F32)

    def body(off):
        part = row_range(off, rows)
        pre = dot(normed_ref[part], joined[...]) * scale_in
        cumul = 0.5 * (1.0 + lax.erf(pre * HALF_ROOT))
        density = jnp.exp(-0.5 * pre * pre) * INV_ROOT_TAU
        hidden = (pre * cumul).astype(BF16)
        slope_ref[part] = (cumul + pre * density).astype(BF16)
        total[...] += dot(hidden, grads_ref[part], (0, 0))

    loop(count, body, first)
    adam_tiles(
        w_ref,
        m_ref,
        v_ref,
        lambda rows: total[rows] * corr_ref[2],
        corr_ref,
        updated_ref,
        first_ref,
        second_ref,
        32,
    )


def hidden_chunk(me, corr, span, normed, grads, w, m, v, wide, low, previous, after):
    count = len(wide)
    total, width = normed.shape
    owned, part = w.shape[0], width // count
    start, size = span
    block = min(BLOCK, size)
    base = start // block
    rows = total // count
    row_block = pl.BlockSpec((block, width), lambda f, *_: (base + f, 0))
    arrays = [array for array, _ in wide]
    wide_specs = [
        pl.BlockSpec((part, block), lambda f, *_, lead=lead: (lead, low // block + f))
        for _, lead in wide
    ]
    if grads is None:
        spread = width // size * rows
        more = [pl.BlockSpec((spread, size), lambda f, *_: (0, 0))] * count
        extra = arrays
        out_grads = [jax.ShapeDtypeStruct((total, width), BF16)]
    else:
        more = [whole(grads)]
        extra = [grads]
        out_grads = []
    chained = previous is not None
    last = 6 + count + len(extra)
    return pl.pallas_call(
        partial(hidden_kernel, count=count, first=grads is None),
        out_shape=[
            jax.ShapeDtypeStruct((size, width), BF16),
            jax.ShapeDtypeStruct(m.shape, F32),
            jax.ShapeDtypeStruct(v.shape, F32),
            jax.ShapeDtypeStruct((total, owned), BF16),
        ]
        + out_grads,
        grid_spec=pltpu.PrefetchScalarGridSpec(
            num_scalar_prefetch=2,
            grid=(size // block,),
            in_specs=[whole(normed), row_block, row_block, row_block]
            + wide_specs
            + more
            + ([hbm()] * 3 if chained else [])
            + [hbm()] * len(after),
            out_specs=[
                pl.BlockSpec((block, width), lambda f, *_: (f, 0)),
                row_block,
                row_block,
                pl.BlockSpec((total, block), lambda f, *_: (0, base + f)),
            ]
            + [whole(g) for g in out_grads],
            scratch_shapes=[pltpu.VMEM((width, block), BF16), pltpu.VMEM((block, width), F32)],
        ),
        input_output_aliases={last: 1, last + 1: 2, last + 2: 3} if chained else {},
        compiler_params=params(20 * MIB + 5 * total * width * 2),
        cost_estimate=cost(),
        name=f"hidden_{start}",
    )(me, corr, normed, w, m, v, *arrays, *extra, *(previous or ()), *after)


def expand_kernel(me_ref, corr_ref, turned_ref, grads_ref, w_ref, slope_ref, *refs, count):
    *outs, pre_ref, scratch = refs[-count - 2 :]
    width = turned_ref.shape[0]
    rows = grads_ref.shape[0] // count
    scale_in = 1.0 / math.sqrt(width)

    def body(off):
        part = row_range(off, rows)
        back = dot(grads_ref[part], w_ref[...], (1, 1)) * corr_ref[2]
        pre_ref[part] = (back * slope_ref[part].astype(F32)).astype(BF16)

    loop(count, body)
    scratch[...] = (dot(turned_ref[...], pre_ref[...]) * scale_in).astype(BF16)
    piece = width // count
    for off in range(count):
        start = pl.multiple_of((me_ref[0] ^ off) * piece, 16)
        outs[off][...] = scratch[pl.ds(start, piece)]


def expand_chunk(me, corr, span, turned, grads, w, slope, count, after):
    width, total = turned.shape
    start, size = span
    block = min(BLOCK, size)
    base = start // block
    piece = width // count
    return pl.pallas_call(
        partial(expand_kernel, count=count),
        out_shape=[jax.ShapeDtypeStruct((piece, size), BF16)] * count
        + [jax.ShapeDtypeStruct((total, size), BF16)],
        grid_spec=pltpu.PrefetchScalarGridSpec(
            num_scalar_prefetch=2,
            grid=(size // block,),
            in_specs=[
                whole(turned),
                whole(grads),
                pl.BlockSpec((block, width), lambda f, *_: (base + f, 0)),
                pl.BlockSpec((total, block), lambda f, *_: (0, base + f)),
            ]
            + [hbm()] * len(after),
            out_specs=[pl.BlockSpec((piece, block), lambda f, *_: (0, f))] * count
            + [pl.BlockSpec((total, block), lambda f, *_: (0, f))],
            scratch_shapes=[pltpu.VMEM((width, block), BF16)],
        ),
        compiler_params=params(20 * MIB + 5 * total * width * 2),
        cost_estimate=cost(),
        name=f"expand_{start}",
    )(me, corr, turned, grads, w, slope, *after)


def update_kernel(me_ref, corr_ref, w_ref, m_ref, v_ref, *refs, count):
    pieces = refs[:count]
    updated_ref, first_ref, second_ref, held = refs[-4:]
    for off in range(count):

        @pl.when(pl.program_id(0) == off)
        def _():
            held[...] = pieces[off][...]

    adam_tiles(
        w_ref,
        m_ref,
        v_ref,
        lambda rows: held[rows].astype(F32),
        corr_ref,
        updated_ref.at[0],
        first_ref,
        second_ref,
        48,
    )


def update_chunk(me, corr, span, w, m, v, pieces, previous, after):
    count = len(pieces)
    rows, size = pieces[0].shape
    start, _ = span
    ratio = w.shape[1] // count // size
    base = start // size
    column = pl.BlockSpec((rows, size), lambda i, me, *_: (0, (me[0] ^ i) * ratio + base))
    chained = previous is not None
    last = 5 + count
    return pl.pallas_call(
        partial(update_kernel, count=count),
        out_shape=[
            jax.ShapeDtypeStruct((count, rows, size), BF16),
            jax.ShapeDtypeStruct(m.shape, F32),
            jax.ShapeDtypeStruct(v.shape, F32),
        ],
        grid_spec=pltpu.PrefetchScalarGridSpec(
            num_scalar_prefetch=2,
            grid=(count,),
            in_specs=[column, column, column]
            + [whole(p) for p in pieces]
            + ([hbm()] * 2 if chained else [])
            + [hbm()] * len(after),
            out_specs=[
                pl.BlockSpec((1, rows, size), lambda i, *_: (i, 0, 0)),
                column,
                column,
            ],
            scratch_shapes=[pltpu.VMEM((rows, size), BF16)],
        ),
        input_output_aliases={last: 1, last + 1: 2} if chained else {},
        compiler_params=params(24 * MIB),
        cost_estimate=cost(),
        name=f"update_{start}",
    )(me, corr, w, m, v, *pieces, *(previous or ()), *after)


def mean_tiles(own_ref, other_ref, out_ref):
    rows = out_ref.shape[0]
    tile = math.gcd(rows, 64)

    def body(i, carry):
        part = pl.ds(pl.multiple_of(i * tile, tile), tile)
        value = (own_ref[part].astype(F32) + other_ref[part].astype(F32)) * 0.5
        out_ref[part] = value.astype(BF16)
        return carry

    lax.fori_loop(0, rows // tile, body, 0)


def mean_project_kernel(*refs, parts):
    out_ref = refs[-1]
    for i, (start, size) in enumerate(parts):
        mean_tiles(refs[2 * i], refs[2 * i + 1], out_ref.at[pl.ds(start, size)])


def mean_project(pairs, parts):
    flat = [x for pair in pairs for x in pair]
    shape = jax.ShapeDtypeStruct((sum(p[0].shape[0] for p in pairs), flat[0].shape[1]), BF16)
    return pl.pallas_call(
        partial(mean_project_kernel, parts=parts),
        out_shape=shape,
        grid=(1,),
        in_specs=[whole(x) for x in flat],
        out_specs=whole(shape),
        compiler_params=params(24 * MIB),
        cost_estimate=cost(),
        name="mean_project",
    )(*flat)


def mean_expand_kernel(me_ref, own_ref, other_ref, *refs):
    mean_tiles(own_ref.at[0], other_ref.at[0], refs[-1])


def mean_expand(me, span, own, other, full, previous, after):
    count, rows, size = own.shape
    ratio = full // count // size
    base = span[0] // size
    in_spec = pl.BlockSpec((1, rows, size), lambda i, m: (i, 0, 0))
    chained = previous is not None
    return pl.pallas_call(
        mean_expand_kernel,
        out_shape=pltpu.HBM((rows, full), BF16),
        grid_spec=pltpu.PrefetchScalarGridSpec(
            num_scalar_prefetch=1,
            grid=(count,),
            in_specs=[in_spec, in_spec] + [hbm()] * (chained + len(after)),
            out_specs=pl.BlockSpec((rows, size), lambda i, m: (0, (m[0] ^ i) * ratio + base)),
        ),
        input_output_aliases={3: 0} if chained else {},
        compiler_params=params(16 * MIB),
        cost_estimate=cost(),
        name=f"mean_expand_{span[0]}",
    )(me, own, other, *((previous,) if chained else ()), *after)


def rows_kernel(me_ref, *refs, count, groups, parts):
    pre = refs[:groups]
    wide = refs[groups : groups + len(parts) * count]
    *outs, joined = refs[-count - 1 :]
    width = joined.shape[0]

    @pl.when(pl.program_id(0) == 0)
    def _():
        for i, (start, size) in enumerate(parts):
            pieces = wide[i * count : (i + 1) * count]
            join_rows(me_ref[0], pieces, joined, slice(start, start + size))

    total = None
    low = 0
    for piece in pre:
        size = piece.shape[1]
        term = dot(piece[...], joined[:, low : low + size], (1, 1))
        total = term if total is None else total + term
        low += size
    total = (total * (1.0 / math.sqrt(width))).astype(BF16)
    for off in range(count):

        @pl.when(pl.program_id(0) == off)
        def _():
            outs[off][...] = total


def row_grads(me, pre, wide, parts, width, after):
    count = len(wide[0])
    total = pre[0].shape[0]
    rows = total // count
    owned = sum(p.shape[1] for p in pre)
    flat = [piece for chunk in wide for piece in chunk]
    shapes = [jax.ShapeDtypeStruct((rows, width), BF16)] * count
    return pl.pallas_call(
        partial(rows_kernel, count=count, groups=len(pre), parts=parts),
        out_shape=shapes,
        grid_spec=pltpu.PrefetchScalarGridSpec(
            num_scalar_prefetch=1,
            grid=(count,),
            in_specs=[pl.BlockSpec((rows, p.shape[1]), lambda i, m: (i, 0)) for p in pre]
            + [
                pl.BlockSpec((width // count, x.shape[1]), lambda i, m, lead=lead: (lead, 0))
                for x, lead in flat
            ]
            + [hbm()] * len(after),
            out_specs=[whole(x) for x in shapes],
            scratch_shapes=[pltpu.VMEM((width, owned), BF16)],
        ),
        compiler_params=params(24 * MIB),
        cost_estimate=cost(),
        name="row_grads",
    )(me, *pre, *[x for x, _ in flat], *after)


def norm_back_kernel(gain_ref, unit_ref, inv_ref, *refs, count, steps, tile):
    pieces = refs[:count]
    conv_ref, first_ref, last_ref = refs[-3:]

    def body(i, carry):
        rows = pl.ds(pl.multiple_of(i * tile, tile), tile)
        total = pieces[0][rows].astype(F32)
        for piece in pieces[1:]:
            total = total + piece[rows].astype(F32)
        scaled = total * gain_ref[...]
        unit = unit_ref[rows]
        conv_ref[rows] = inv_ref[rows, :1] * (
            scaled
            - jnp.mean(scaled, axis=-1, keepdims=True)
            - unit * jnp.mean(scaled * unit, axis=-1, keepdims=True)
        )
        return carry

    lax.fori_loop(0, conv_ref.shape[0] // tile, body, 0)
    for s in range(first_ref.shape[0]):
        first_ref[s] = conv_ref[s * steps : s * steps + PAD].astype(BF16)
        last_ref[s] = conv_ref[(s + 1) * steps - PAD : (s + 1) * steps].astype(BF16)


def norm_back(gain, unit, inv, pieces, seqs, steps, after):
    count = len(pieces)
    width = unit.shape[1]
    edge = jax.ShapeDtypeStruct((seqs, PAD, width), BF16)
    full = jax.ShapeDtypeStruct((seqs * steps, width), F32)
    return pl.pallas_call(
        partial(norm_back_kernel, count=count, steps=steps, tile=32),
        out_shape=[full, edge, edge],
        grid=(1,),
        in_specs=[whole(gain), whole(unit), whole(inv)]
        + [whole(p) for p in pieces]
        + [hbm()] * len(after),
        out_specs=[whole(full), whole(edge), whole(edge)],
        compiler_params=params(32 * MIB),
        cost_estimate=cost(),
        name="norm_back",
    )(gain, unit, inv, *pieces, *after)


def conv_back_kernel(taps_ref, grad_ref, low_ref, high_ref, cot_ref, out_ref, padded, *, tile):
    seqs, steps, width = out_ref.shape
    taps = taps_ref.shape[0]
    reach = taps // 2
    for s in range(seqs):
        padded[s, :PAD] = low_ref[s].astype(F32)
        padded[s, PAD + steps :] = high_ref[s].astype(F32)

    def fill(i, carry):
        s = i // (steps // tile)
        r = i % (steps // tile)
        rows = pl.ds(pl.multiple_of(i * tile, tile), tile)
        padded[s, pl.ds(pl.multiple_of(r * tile + PAD, 8), tile)] = grad_ref[rows]
        return carry

    def body(i, carry):
        s = i // (steps // tile)
        r = i % (steps // tile)
        rows = pl.ds(pl.multiple_of(r * tile, tile), tile)
        window = padded.at[s, pl.ds(pl.multiple_of(r * tile, 8), tile + 2 * PAD)]
        back = cot_ref[pl.ds(pl.multiple_of(i * tile, tile), tile)].astype(F32)
        for j in range(taps):
            low = PAD + reach - j
            back = back + taps_ref[j : j + 1] * window[low : low + tile]
        out_ref[s, rows] = back.astype(BF16)
        return carry

    lax.fori_loop(0, seqs * steps // tile, fill, 0)
    lax.fori_loop(0, seqs * steps // tile, body, 0)


def conv_back(taps, grad, low, high, cot, seqs):
    total, width = cot.shape
    steps = total // seqs
    shape = jax.ShapeDtypeStruct((seqs, steps, width), BF16)
    return pl.pallas_call(
        partial(conv_back_kernel, tile=32),
        out_shape=shape,
        grid=(1,),
        in_specs=[whole(x) for x in (taps, grad, low, high, cot)],
        out_specs=whole(shape),
        scratch_shapes=[pltpu.VMEM((seqs, steps + 2 * PAD, width), F32)],
        compiler_params=params(32 * MIB),
        cost_estimate=cost(),
        name="conv_back",
    )(taps, grad, low, high, cot)


def step(
    series,
    cotangent,
    observed,
    depth_kernel,
    norm_gain,
    layer_scale,
    step_index,
    w_expand,
    w_project,
    first_expand,
    second_expand,
    first_project,
    second_project,
    level,
):
    count = lax.axis_size("fsdp")
    seqs, steps, width = series.shape[1:]
    rows = seqs * steps
    hidden_width = w_expand.shape[2]
    owned = hidden_width // count
    sent, parts, groups = plan(owned)
    me = lax.axis_index("fsdp").astype(jnp.int32).reshape(1)
    gain = norm_gain.reshape(1, width)
    we, wp = w_expand[0], w_project[0]
    me_ax, ve_ax = first_expand[0], second_expand[0]
    mp_ax, vp_ax = first_project[0], second_project[0]

    timestep = (step_index[0] + 1).astype(F32)
    corr = jnp.stack(
        [
            1.0 / (1.0 - jnp.power(F32(BETA_ONE), timestep)),
            1.0 / (1.0 - jnp.power(F32(BETA_TWO), timestep)),
            F32(1.0 / math.sqrt(hidden_width)),
        ]
    )

    part = width // count
    first_spans = [span for span in parts if sum(span) <= sum(sent[0])]
    spans = first_spans + list(sent[1:])
    seen = observed[0].reshape(rows, 1).astype(F32)
    cot = cotangent[0].reshape(rows, width)
    packs, masked = pack_first(
        me, cot, seen, layer_scale.reshape(1, width), we, count, first_spans
    )
    series_pieces = gather_xor(series[0], (packs[0],))
    normed, turned, unit, inv = norm_rows(me, series_pieces, depth_kernel, gain, ())
    base = width // parts[0][1] * rows // part
    held = relay_packs(send_packs(packs), (normed,))
    wide = [pieces_of(held, base, len(first_spans), k) for k in range(len(first_spans))]
    received = [send_packs(slice_weights(me, we, count, span)) for span in sent[1:]]

    project_pairs = []
    expand_pairs = []
    pre = []
    carried = None
    grads = None
    done = 0
    pending = list(groups)
    for i, (start, size) in enumerate(parts):
        if i == 0:
            after = ()
        elif i == 2:
            after = (token(project_pairs[0][1], "first_arrived"), *pre)
        else:
            after = ()
        at = max(j for j, (low, _) in enumerate(spans) if low <= start)
        low = start - spans[at][0]
        updated, *carried = hidden_chunk(
            me, corr, (start, size), normed, grads, wp, mp_ax, vp_ax, wide[at], low, carried, after
        )
        if i == 0:
            grads = carried.pop()
        if i == 1:
            wide += [pieces_of(relay_packs(packs, (updated,)), 0, 1, 0) for packs in received]
        project_pairs.append((updated, swap_gossip(updated, level)))
        done = start + size
        while pending and sum(pending[0]) <= done:
            after = (project_pairs[1][1], expand_pairs[0][-1]) if len(pre) else ()
            *blocks, pre_g = expand_chunk(
                me, corr, pending.pop(0), turned, grads, wp, carried[2], count, after
            )
            pre.append(pre_g)
            expand_pairs.append(swap_blocks(blocks))
    first_project_next, second_project_next, _ = carried

    moments = None
    for i, span in enumerate(groups):
        last = i + 1 == len(groups)
        if last:
            back = row_grads(me, pre, wide, spans, width, tuple(u for u, _ in expand_pairs[:i]))
            after = (*(other for _, other in project_pairs[2:]), back[0])
        else:
            after = ()
        updated, *moments = update_chunk(
            me, corr, span, we, me_ax, ve_ax, expand_pairs[i], moments, after
        )
        expand_pairs[i] = (updated, swap_gossip(updated, level))
    first_expand_next, second_expand_next = moments

    back_pieces = swap_blocks(back)

    after = tuple(other for _, other in expand_pairs[:-1])
    grad_conv, first_rows, last_rows = norm_back(
        gain, unit, inv, back_pieces, seqs, steps, after
    )
    forward = [(i, i + 1) for i in range(count - 1)]
    backward = [(target, source) for source, target in forward]
    low = lax.ppermute(last_rows, "fsdp", forward)
    high = lax.ppermute(first_rows, "fsdp", backward)
    input_grad = conv_back(depth_kernel, grad_conv, low, high, masked, seqs)

    shared_project = mean_project(project_pairs, parts)
    shared_expand = None
    for span, pair in zip(groups, expand_pairs):
        after = (input_grad, shared_project) if shared_expand is None else ()
        shared_expand = mean_expand(me, span, *pair, hidden_width, shared_expand, after)
    return (
        shared_expand[None],
        shared_project[None],
        first_expand_next[None],
        second_expand_next[None],
        first_project_next[None],
        second_project_next[None],
        input_grad[None],
    )


def body(*args):
    step_index = args[6]
    levels = lax.axis_size("gossip").bit_length() - 1
    return lax.switch(
        step_index[0] % levels,
        [lambda *a, level=level: step(*a, level) for level in range(levels)],
        *args,
    )


def solution(mesh):
    rows = P("gossip", "fsdp", None)
    steps = P("gossip", None, "fsdp", None)
    in_specs = (steps, steps, P("gossip", None, "fsdp"), P(), P(), P(), P()) + (rows,) * 6
    out_specs = (rows,) * 6 + (steps,)
    return jax.shard_map(body, mesh=mesh, in_specs=in_specs, out_specs=out_specs, check_vma=False)
```

profile of v0, /device:TPU:1, one launch (start us, length us, event | category | flops | bytes accessed | tf_op | source)
XLA Modules:
  0.0 117.6 jit_solution(1839868093437194530)
XLA Ops:
  1.3 116.3 %conditional.1 = (bf16[1,192,4096]{2,1,0:T(8,128)(2,1)}, bf16[1,1024,768]{2,1,0:T(8,128)(2,1)}, f32[1,192,4096]{2,1,0:T(8,128)}, f32[1,192,4096]{2,1,0:T(8,128)}...) conditional(s32[]{:T(128)} %clamp.3, (s32[1]{0:T(128)}, ...), branch_computations={%region_0.1_spmd, %region_1.2_spmd, %region_2.3_spmd} | conditional | flops 288 | bytes 247776800 | solution.py:868
  1.5 2.1 %collective-permute-start.27 = (bf16[2,128,768]{2,1,0:T(8,128)(2,1)}, bf16[2,128,768]{2,1,0:T(8,128)(2,1)S(1)}, u32[]{:S(2)}, u32[]{:S(2)}) collective-permute-start(bf16[2,128,768]{2,1,0:T(8,128)(2,1)} %bitcast.175), channel_id=1, source_target_pairs={{0,2},{1,3},{2,0},{3,1},{4,6},{5,7},{6,4},{7,5},{8,10},{9,11},{10,... | collective-permute-start | bytes 1179656 | tf_op jit(solution)/shard_map/cond/branch_1_fun/ppermute | solution.py:78
  3.6 0.7 convert_element_type.22
  4.3 0.7 reshape.111.scale_ref
  5.0 0.1 copy.78.seen_ref
  5.1 0.0 copy-start.37
  5.2 0.0 copy-start.43
  5.2 0.0 copy-start.40
  5.2 0.0 copy-start.1
  5.2 1.7 %pack_first.4 = (bf16[1536,256]{1,0:T(8,128)(2,1)S(1)}, bf16[1536,256]{1,0:T(8,128)(2,1)S(1)}, bf16[256,768]{1,0:T(8,128)(2,1)S(1)}) custom-call(s32[1]{0:T(128)} %bitcast.17.me_ref, bf16[256,768]{1,0:T(8,128)(2,1)} %bitcast.170, f32[256,1]{1,0:T(8,128)S(1)} %copy.78.seen_ref, f32[1,768]{1,0:T(1,128)S(1)} %reshape.111.scale_ref, bf16[192,4096]{1,0:T(8,128)(2,1)} %bitcast.66, ...), custom_call_target="tpu_custom_call" | custom-call | flops 1 | bytes 1 | tf_op jit(solution)/shard_map/cond/branch_1_fun/pack_first/pallas_call | solution.py:197
  6.9 0.1 collective-permute-start.30
  7.0 1.0 collective-permute-start.26
  8.0 4.7 %collective-permute-done.27.refs_2_ = bf16[2,128,768]{2,1,0:T(8,128)(2,1)S(1)} collective-permute-done((bf16[2,128,768]{2,1,0:T(8,128)(2,1)}, bf16[2,128,768]{2,1,0:T(8,128)(2,1)S(1)}, u32[]{:S(2)}, u32[]{:S(2)}) %collective-permute-start.27) | collective-permute-done | bytes 393248 | tf_op jit(solution)/shard_map/cond/branch_1_fun/ppermute | solution.py:78
  12.7 2.1 %collective-permute-start.28 = (bf16[2,128,768]{2,1,0:T(8,128)(2,1)S(1)}, bf16[2,128,768]{2,1,0:T(8,128)(2,1)S(1)}, u32[]{:S(2)}, u32[]{:S(2)}) collective-permute-start(bf16[2,128,768]{2,1,0:T(8,128)(2,1)S(1)} %collective-permute-done.27.refs_2_), channel_id=1, source_target_pairs={{0,1},{1,0},{2,3},{3,2},{4,5},{5,4},{6,7},{7,6},{8,9},{9,8},{10,11... | collective-permute-start | bytes 1179656 | tf_op jit(solution)/shard_map/cond/branch_1_fun/ppermute | solution.py:78
  14.8 1.3 %collective-permute-done.28.refs_3_ = bf16[2,128,768]{2,1,0:T(8,128)(2,1)S(1)} collective-permute-done((bf16[2,128,768]{2,1,0:T(8,128)(2,1)S(1)}, bf16[2,128,768]{2,1,0:T(8,128)(2,1)S(1)}, u32[]{:S(2)}, u32[]{:S(2)}) %collective-permute-start.28) | collective-permute-done | bytes 393248 | tf_op jit(solution)/shard_map/cond/branch_1_fun/ppermute | solution.py:78
  16.1 6.1 %norm_rows.4 = (bf16[1024,768]{1,0:T(8,128)(2,1)S(1)}, bf16[768,1024]{1,0:T(8,128)(2,1)S(1)}, f32[256,768]{1,0:T(8,128)S(1)}, f32[256,128]{1,0:T(8,128)S(1)}) custom-call(s32[1]{0:T(128)} %bitcast.17.me_ref, f32[7,768]{1,0:T(8,128)S(1)} %copy-done.40, f32[1,768]{1,0:T(1,128)S(1)} %reshape.110.gain_ref, bf16[2,128,768]{2,1,0:T(8,128)(2,1)S(1)} %bitcast.177, ...), custom_call_target="tpu_custom_call" | custom-call | flops 1 | bytes 41943040 | tf_op jit(solution)/shard_map/cond/branch_1_fun/norm_rows/pallas_call | solution.py:263
  22.2 7.3 %collective-permute-done.30.refs_2_.refs_6_.refs_4_.refs_8_ = bf16[1536,256]{1,0:T(8,128)(2,1)S(1)} collective-permute-done((bf16[1536,256]{1,0:T(8,128)(2,1)S(1)}, bf16[1536,256]{1,0:T(8,128)(2,1)S(1)}, u32[]{:S(2)}, u32[]{:S(2)}) %collective-permute-start.30) | collective-permute-done | bytes 786464 | tf_op jit(solution)/shard_map/cond/branch_1_fun/ppermute | solution.py:78
  29.5 1.2 %collective-permute-start.31 = (bf16[1536,256]{1,0:T(8,128)(2,1)S(1)}, bf16[1536,256]{1,0:T(8,128)(2,1)S(1)}, u32[]{:S(2)}, u32[]{:S(2)}) collective-permute-start(bf16[1536,256]{1,0:T(8,128)(2,1)S(1)} %collective-permute-done.30.refs_2_.refs_6_.refs_4_.refs_8_), channel_id=1, source_target_pairs={{0,1},{1,0},{2,3},{3,2},{4,5},{5,4},{6,7},{7,6},{8,9},{9,8},{10,11... | collective-permute-start | bytes 2359304 | tf_op jit(solution)/shard_map/cond/branch_1_fun/ppermute | solution.py:78
  30.8 0.1 slice_512.4
  30.8 1.5 %collective-permute-start.33 = (bf16[384,512]{1,0:T(8,128)(2,1)S(1)}, bf16[384,512]{1,0:T(8,128)(2,1)S(1)}, u32[]{:S(2)}, u32[]{:S(2)}) collective-permute-start(bf16[384,512]{1,0:T(8,128)(2,1)S(1)} %get-tuple-element.164), channel_id=1, source_target_pairs={{0,2},{1,3},{2,0},{3,1},{4,6},{5,7},{6,4},{7,5},{8,10},{9,11},{10,... | collective-permute-start | bytes 1179656 | tf_op jit(solution)/shard_map/cond/branch_1_fun/ppermute | solution.py:78
  32.4 0.3 collective-permute-start.32
  33.5 0.1 pad_maximum_fusion.1.corr_ref
  33.6 3.0 %hidden_0.4 = (bf16[256,768]{1,0:T(8,128)(2,1)S(1)}, f32[1024,768]{1,0:T(8,128)S(1)}, f32[1024,768]{1,0:T(8,128)S(1)}, bf16[1024,1024]{1,0:T(8,128)(2,1)S(1)}, bf16[1024,768]{1,0:T(8,128)(2,1)S(1)}) custom-call(s32[1]{0:T(128)} %bitcast.17.me_ref, f32[3]{0:T(128)S(1)} %pad_maximum_fusion.1.corr_ref, bf16[1024,768]{1,0:T(8,128)(2,1)S(1)} %get-tuple-element.156.normed_ref, ...), custom_call_target="tpu_custom_call" | custom-call | flops 1 | bytes 1 | tf_op jit(solution)/shard_map/cond/branch_1_fun/hidden_0/pallas_call | solution.py:390
  36.5 1.4 %collective-permute-start.35 = (bf16[256,768]{1,0:T(8,128)(2,1)S(1)}, bf16[256,768]{1,0:T(8,128)(2,1)S(1)}, u32[]{:S(2)}, u32[]{:S(2)}) collective-permute-start(bf16[256,768]{1,0:T(8,128)(2,1)S(1)} %get-tuple-element.173.refs_0_), channel_id=1, source_target_pairs={{0,8},{4,12},{8,0},{12,4},{16,24},{20,28},{24,16},{28,20},{1,9},{5... | collective-permute-start | bytes 1179656 | tf_op jit(solution)/shard_map/cond/branch_1_fun/ppermute | solution.py:117
  37.9 4.5 %hidden_256.4 = (bf16[256,768]{1,0:T(8,128)(2,1)S(1)}, f32[1024,768]{1,0:T(8,128)S(1)}, f32[1024,768]{1,0:T(8,128)S(1)}, bf16[1024,1024]{1,0:T(8,128)(2,1)S(1)}) custom-call(s32[1]{0:T(128)} %bitcast.17.me_ref, f32[3]{0:T(128)S(1)} %pad_maximum_fusion.1.corr_ref, ...), custom_call_target="tpu_custom_call", output_to_operand_aliasing={{1}: (11, {}), {2}: (12, {}), {3}: (13, {})} | custom-call | flops 1 | bytes 1 | tf_op jit(solution)/shard_map/cond/branch_1_fun/hidden_256/pallas_call | solution.py:390
  42.4 0.6 collective-permute-start.34
  43.0 0.9 collective-permute-start.36
  44.0 4.6 %expand_0.4 = (bf16[192,512]{1,0:T(8,128)(2,1)S(1)}, bf16[192,512]{1,0:T(8,128)(2,1)S(1)}, bf16[192,512]{1,0:T(8,128)(2,1)S(1)}, bf16[192,512]{1,0:T(8,128)(2,1)S(1)}, bf16[1024,512]{1,0:T(8,128)(2,1)S(1)}) custom-call(s32[1]{0:T(128)} %bitcast.17.me_ref, f32[3]{0:T(128)S(1)} %pad_maximum_fusion.1.corr_ref, ...), custom_call_target="tpu_custom_call" | custom-call | flops 1 | bytes 1 | tf_op jit(solution)/shard_map/cond/branch_1_fun/expand_0/pallas_call | solution.py:448
  48.5 1.5 %collective-permute-start.37 = (bf16[192,512]{1,0:T(8,128)(2,1)S(1)}, bf16[192,512]{1,0:T(8,128)(2,1)S(1)}, u32[]{:S(2)}, u32[]{:S(2)}) collective-permute-start(bf16[192,512]{1,0:T(8,128)(2,1)S(1)} %get-tuple-element.179), channel_id=1, source_target_pairs={{0,3},{1,2},{2,1},{3,0},{4,7},{5,6},{6,5},{7,4},{8,11},{9,10},{10,... | collective-permute-start | bytes 589832 | tf_op jit(solution)/shard_map/cond/branch_1_fun/ppermute | solution.py:78
  50.0 0.2 collective-permute-start.41
  50.2 0.2 collective-permute-start.42
  50.5 4.5 %hidden_512.4 = (bf16[256,768]{1,0:T(8,128)(2,1)S(1)}, f32[1024,768]{1,0:T(8,128)S(1)}, f32[1024,768]{1,0:T(8,128)S(1)}, bf16[1024,1024]{1,0:T(8,128)(2,1)S(1)}) custom-call(s32[1]{0:T(128)} %bitcast.17.me_ref, f32[3]{0:T(128)S(1)} %pad_maximum_fusion.1.corr_ref, ...), custom_call_target="tpu_custom_call", output_to_operand_aliasing={{1}: (11, {}), {2}: (12, {}), {3}: (13, {})} | custom-call | flops 1 | bytes 1 | tf_op jit(solution)/shard_map/cond/branch_1_fun/hidden_512/pallas_call | solution.py:390
  55.0 4.5 %hidden_768.4 = (bf16[256,768]{1,0:T(8,128)(2,1)S(1)}, f32[1024,768]{1,0:T(8,128)S(1)}, f32[1024,768]{1,0:T(8,128)S(1)}, bf16[1024,1024]{1,0:T(8,128)(2,1)S(1)}) custom-call(s32[1]{0:T(128)} %bitcast.17.me_ref, f32[3]{0:T(128)S(1)} %pad_maximum_fusion.1.corr_ref, ...), custom_call_target="tpu_custom_call", output_to_operand_aliasing={{1}: (11, {}), {2}: (12, {}), {3}: (13, {})} | custom-call | flops 1 | bytes 1 | tf_op jit(solution)/shard_map/cond/branch_1_fun/hidden_768/pallas_call | solution.py:390
  59.5 0.0 copy-start.13
  59.6 0.0 copy-start.16
  59.6 0.6 collective-permute-start.44
  60.2 0.9 collective-permute-start.43
  61.1 4.6 %expand_512.4 = (bf16[192,512]{1,0:T(8,128)(2,1)S(1)}, bf16[192,512]{1,0:T(8,128)(2,1)S(1)}, bf16[192,512]{1,0:T(8,128)(2,1)S(1)}, bf16[192,512]{1,0:T(8,128)(2,1)S(1)}, bf16[1024,512]{1,0:T(8,128)(2,1)S(1)}) custom-call(s32[1]{0:T(128)} %bitcast.17.me_ref, f32[3]{0:T(128)S(1)} %pad_maximum_fusion.1.corr_ref, ...), custom_call_target="tpu_custom_call" | custom-call | flops 1 | bytes 1 | tf_op jit(solution)/shard_map/cond/branch_1_fun/expand_512/pallas_call | solution.py:448
  65.7 1.2 %collective-permute-start.38 = (bf16[192,512]{1,0:T(8,128)(2,1)S(1)}, bf16[192,512]{1,0:T(8,128)(2,1)S(1)}, u32[]{:S(2)}, u32[]{:S(2)}) collective-permute-start(bf16[192,512]{1,0:T(8,128)(2,1)S(1)} %get-tuple-element.181), channel_id=1, source_target_pairs={{0,1},{1,0},{2,3},{3,2},{4,5},{5,4},{6,7},{7,6},{8,9},{9,8},{10,11... | collective-permute-start | bytes 589832 | tf_op jit(solution)/shard_map/cond/branch_1_fun/ppermute | solution.py:78
  66.9 1.3 %collective-permute-start.39 = (bf16[192,512]{1,0:T(8,128)(2,1)S(1)}, bf16[192,512]{1,0:T(8,128)(2,1)S(1)}, u32[]{:S(2)}, u32[]{:S(2)}) collective-permute-start(bf16[192,512]{1,0:T(8,128)(2,1)S(1)} %get-tuple-element.182), channel_id=1, source_target_pairs={{0,2},{1,3},{2,0},{3,1},{4,6},{5,7},{6,4},{7,5},{8,10},{9,11},{10,... | collective-permute-start | bytes 589832 | tf_op jit(solution)/shard_map/cond/branch_1_fun/ppermute | solution.py:78
  68.2 0.5 collective-permute-start.40
  68.6 2.9 %update_0.4 = (bf16[4,192,512]{2,1,0:T(8,128)(2,1)S(1)}, f32[192,4096]{1,0:T(8,128)S(1)}, f32[192,4096]{1,0:T(8,128)S(1)}) custom-call(s32[1]{0:T(128)} %bitcast.17.me_ref, f32[3]{0:T(128)S(1)} %pad_maximum_fusion.1.corr_ref, bf16[192,4096]{1,0:T(8,128)(2,1)S(1)} %bitcast.78, f32[192,4096]{1,0:T(8,128)S(1)} %bitcast.144, f32[192,4096]{1,0:T(8,128)S(1)} %bitcast.150, ...), custom_call_target="tpu_custom_call" | custom-call | flops 1 | bytes 1 | tf_op jit(solution)/shard_map/cond/branch_1_fun/update_0/pallas_call | solution.py:503
  71.6 0.7 collective-permute-start.46
  72.3 3.0 %row_grads.4 = (bf16[256,768]{1,0:T(8,128)(2,1)S(1)}, bf16[256,768]{1,0:T(8,128)(2,1)S(1)}, bf16[256,768]{1,0:T(8,128)(2,1)S(1)}, bf16[256,768]{1,0:T(8,128)(2,1)S(1)}) custom-call(s32[1]{0:T(128)} %bitcast.17.me_ref, bf16[1024,512]{1,0:T(8,128)(2,1)S(1)} %get-tuple-element.174.refs_9_.refs_0_, bf16[1024,512]{1,0:T(8,128)(2,1)S(1)} %get-tuple-element.191.refs_1_, ...), custom_call_target="tpu_custom_call" | custom-call | flops 1 | bytes 1 | tf_op jit(solution)/shard_map/cond/branch_1_fun/row_grads/pallas_call | solution.py:625
  75.2 2.8 %collective-permute-done.40.refs_3_ = bf16[192,512]{1,0:T(8,128)(2,1)S(1)} collective-permute-done((bf16[192,512]{1,0:T(8,128)(2,1)S(1)}, bf16[192,512]{1,0:T(8,128)(2,1)S(1)}, u32[]{:S(2)}, u32[]{:S(2)}) %collective-permute-start.40) | collective-permute-done | bytes 196640 | tf_op jit(solution)/shard_map/cond/branch_1_fun/ppermute | solution.py:78
  78.1 0.1 collective-permute-done.43.refs_6_.refs_5_
  78.1 2.9 %update_512.4 = (bf16[4,192,512]{2,1,0:T(8,128)(2,1)S(1)}, f32[192,4096]{1,0:T(8,128)S(1)}, f32[192,4096]{1,0:T(8,128)S(1)}) custom-call(s32[1]{0:T(128)} %bitcast.17.me_ref, f32[3]{0:T(128)S(1)} %pad_maximum_fusion.1.corr_ref, bf16[192,4096]{1,0:T(8,128)(2,1)S(1)} %bitcast.79, ...), custom_call_target="tpu_custom_call", output_to_operand_aliasing={{1}: (9, {}), {2}: (10, {})} | custom-call | flops 1 | bytes 1 | tf_op jit(solution)/shard_map/cond/branch_1_fun/update_512/pallas_call | solution.py:503
  81.1 0.0 copy-start.25
  81.1 0.6 collective-permute-start.45
  81.7 2.8 %collective-permute-start.47 = (bf16[256,768]{1,0:T(8,128)(2,1)S(1)}, bf16[256,768]{1,0:T(8,128)(2,1)S(1)}, u32[]{:S(2)}, u32[]{:S(2)}) collective-permute-start(bf16[256,768]{1,0:T(8,128)(2,1)S(1)} %get-tuple-element.197), channel_id=1, source_target_pairs={{0,1},{1,0},{2,3},{3,2},{4,5},{5,4},{6,7},{7,6},{8,9},{9,8},{10,11... | collective-permute-start | bytes 1179656 | tf_op jit(solution)/shard_map/cond/branch_1_fun/ppermute | solution.py:78
  84.5 0.8 collective-permute-start.48
  85.4 0.8 collective-permute-start.49
  86.2 9.1 %collective-permute-done.48.refs_2_ = bf16[256,768]{1,0:T(8,128)(2,1)S(1)} collective-permute-done((bf16[256,768]{1,0:T(8,128)(2,1)S(1)}, bf16[256,768]{1,0:T(8,128)(2,1)S(1)}, u32[]{:S(2)}, u32[]{:S(2)}) %collective-permute-start.48) | collective-permute-done | bytes 393248 | tf_op jit(solution)/shard_map/cond/branch_1_fun/ppermute | solution.py:78
  95.3 8.8 %collective-permute-done.49.refs_3_ = bf16[256,768]{1,0:T(8,128)(2,1)S(1)} collective-permute-done((bf16[256,768]{1,0:T(8,128)(2,1)S(1)}, bf16[256,768]{1,0:T(8,128)(2,1)S(1)}, u32[]{:S(2)}, u32[]{:S(2)}) %collective-permute-start.49) | collective-permute-done | bytes 393248 | tf_op jit(solution)/shard_map/cond/branch_1_fun/ppermute | solution.py:78
  104.1 1.2 %norm_back.4 = (f32[256,768]{1,0:T(8,128)S(1)}, bf16[2,8,768]{2,1,0:T(8,128)(2,1)S(1)}, bf16[2,8,768]{2,1,0:T(8,128)(2,1)S(1)}) custom-call(f32[1,768]{1,0:T(1,128)S(1)} %reshape.110.gain_ref, f32[256,768]{1,0:T(8,128)S(1)} %get-tuple-element.195.unit_ref, f32[256,128]{1,0:T(8,128)S(1)} %get-tuple-element.196.inv_ref, ...), custom_call_target="tpu_custom_call" | custom-call | flops 1 | bytes 1 | tf_op jit(solution)/shard_map/cond/branch_1_fun/norm_back/pallas_call | solution.py:675
  105.3 2.6 %collective-permute-start.50 = (bf16[2,8,768]{2,1,0:T(8,128)(2,1)S(1)}, bf16[2,8,768]{2,1,0:T(8,128)(2,1)S(1)}, u32[]{:S(2)}, u32[]{:S(2)}) collective-permute-start(bf16[2,8,768]{2,1,0:T(8,128)(2,1)S(1)} %get-tuple-element.201), channel_id=1, source_target_pairs={{0,1},{1,2},{2,3},{4,5},{5,6},{6,7},{8,9},{9,10},{10,11},{12,13},{... | collective-permute-start | bytes 73736 | tf_op jit(solution)/shard_map/cond/branch_1_fun/ppermute | solution.py:845
  107.9 1.9 %collective-permute-start.51 = (bf16[2,8,768]{2,1,0:T(8,128)(2,1)S(1)}, bf16[2,8,768]{2,1,0:T(8,128)(2,1)S(1)}, u32[]{:S(2)}, u32[]{:S(2)}) collective-permute-start(bf16[2,8,768]{2,1,0:T(8,128)(2,1)S(1)} %get-tuple-element.202), channel_id=1, source_target_pairs={{1,0},{2,1},{3,2},{5,4},{6,5},{7,6},{9,8},{10,9},{11,10},{13,12},{... | collective-permute-start | bytes 73736 | tf_op jit(solution)/shard_map/cond/branch_1_fun/ppermute | solution.py:846
  109.9 0.6 mean_project.4.refs_1_
  110.5 0.0 copy-start.31
  110.5 2.6 %collective-permute-done.51.high_ref = bf16[2,8,768]{2,1,0:T(8,128)(2,1)S(1)} collective-permute-done((bf16[2,8,768]{2,1,0:T(8,128)(2,1)S(1)}, bf16[2,8,768]{2,1,0:T(8,128)(2,1)S(1)}, u32[]{:S(2)}, u32[]{:S(2)}) %collective-permute-start.51) | collective-permute-done | bytes 24608 | tf_op jit(solution)/shard_map/cond/branch_1_fun/ppermute | solution.py:846
  113.1 1.2 %conv_back.4.refs_0_ = bf16[2,128,768]{2,1,0:T(8,128)(2,1)S(1)} custom-call(f32[7,768]{1,0:T(8,128)S(1)} %copy-done.40, f32[256,768]{1,0:T(8,128)S(1)} %get-tuple-element.200.grad_ref, bf16[2,8,768]{2,1,0:T(8,128)(2,1)S(1)} %collective-permute-done.50.low_ref, bf16[2,8,768]{2,1,0:T(8,128)(2,1)S(1)} %collective-permute-done.51.high_ref, ...), custom_call_target="tpu_custom_call" | custom-call | flops 1 | bytes 1 | tf_op jit(solution)/shard_map/cond/branch_1_fun/conv_back/pallas_call | solution.py:724
  114.3 0.0 copy-start.34
  114.3 1.6 %mean_expand_0.4.refs_0_ = bf16[192,4096]{1,0:T(8,128)(2,1)} custom-call(s32[1]{0:T(128)} %bitcast.17.me_ref, bf16[4,192,512]{2,1,0:T(8,128)(2,1)S(1)} %get-tuple-element.192.refs_14_.own_ref, bf16[4,192,512]{2,1,0:T(8,128)(2,1)S(1)} %collective-permute-done.46.refs_4_.other_ref, bf16[2,128,768]{2,1,0:T(8,128)(2,1)S(1)} %conv_back.4.refs_0_, ...), custom_call_target="tpu_custom_call" | custom-call | flops 1 | bytes 1 | tf_op jit(solution)/shard_map/cond/branch_1_fun/mean_expand_0/pallas_call | solution.py:575
  116.0 1.6 %mean_expand_512.4 = bf16[192,4096]{1,0:T(8,128)(2,1)} custom-call(s32[1]{0:T(128)} %bitcast.17.me_ref, bf16[4,192,512]{2,1,0:T(8,128)(2,1)S(1)} %get-tuple-element.194.own_ref, bf16[4,192,512]{2,1,0:T(8,128)(2,1)S(1)} %collective-permute-done.45.other_ref, bf16[192,4096]{1,0:T(8,128)(2,1)} %mean_expand_0.4.refs_0_), custom_call_target="tpu_custom_call", output_to_operand_aliasing={{}: (3, {})} | custom-call | flops 1 | bytes 1 | tf_op jit(solution)/shard_map/cond/branch_1_fun/mean_expand_512/pallas_call | solution.py:575
  (42 shorter events, 0.1 us)
Async XLA Ops:
  1.5 11.2 %collective-permute-start.27 = (bf16[2,128,768]{2,1,0:T(8,128)(2,1)}, bf16[2,128,768]{2,1,0:T(8,128)(2,1)S(1)}, u32[]{:S(2)}, u32[]{:S(2)}) collective-permute-start(bf16[2,128,768]{2,1,0:T(8,128)(2,1)} %bitcast.175), channel_id=1, source_target_pairs={{0,2},{1,3},{2,0},{3,1},{4,6},{5,7},{6,4},{7,5},{8,10},{9,11},{10,... | collective-permute-start | bytes 1179656 | tf_op jit(solution)/shard_map/cond/branch_1_fun/ppermute | solution.py:78
  5.1 1.8 %copy-start.37 = (bf16[1,2,128,768]{3,2,1,0:T(8,128)(2,1)S(1)}, bf16[1,2,128,768]{3,2,1,0:T(8,128)(2,1)}, u32[]{:S(2)}) copy-start(bf16[1,2,128,768]{3,2,1,0:T(8,128)(2,1)} %get-tuple-element.149) | copy-start | bytes 1179652 | tf_op jit(solution)/shard_map/cond
  5.2 9.6 %copy-start.43 = (f32[768]{0:T(1024)S(1)}, f32[768]{0:T(1024)}, u32[]{:S(2)}) copy-start(f32[768]{0:T(1024)} %get-tuple-element.148) | copy-start | bytes 9220 | tf_op jit(solution)/shard_map/cond
  5.2 10.9 %copy-start.40 = (f32[7,768]{1,0:T(8,128)S(1)}, f32[7,768]{1,0:T(8,128)}, u32[]{:S(2)}) copy-start(f32[7,768]{1,0:T(8,128)} %get-tuple-element.147.taps_ref) | copy-start | bytes 64516 | tf_op jit(solution)/shard_map/cond
  5.2 25.6 %copy-start.1 = (bf16[1,192,4096]{2,1,0:T(8,128)(2,1)S(1)}, bf16[1,192,4096]{2,1,0:T(8,128)(2,1)}, u32[]{:S(2)}) copy-start(bf16[1,192,4096]{2,1,0:T(8,128)(2,1)} %get-tuple-element.144) | copy-start | bytes 4718596 | tf_op jit(solution)/shard_map/cond
  6.9 22.6 %collective-permute-start.30 = (bf16[1536,256]{1,0:T(8,128)(2,1)S(1)}, bf16[1536,256]{1,0:T(8,128)(2,1)S(1)}, u32[]{:S(2)}, u32[]{:S(2)}) collective-permute-start(bf16[1536,256]{1,0:T(8,128)(2,1)S(1)} %get-tuple-element.160), channel_id=1, source_target_pairs={{0,2},{1,3},{2,0},{3,1},{4,6},{5,7},{6,4},{7,5},{8,10},{9,11},{10,... | collective-permute-start | bytes 2359304 | tf_op jit(solution)/shard_map/cond/branch_1_fun/ppermute | solution.py:78
  7.0 7.8 %collective-permute-start.26 = (bf16[2,128,768]{2,1,0:T(8,128)(2,1)S(1)}, bf16[2,128,768]{2,1,0:T(8,128)(2,1)S(1)}, u32[]{:S(2)}, u32[]{:S(2)}) collective-permute-start(bf16[2,128,768]{2,1,0:T(8,128)(2,1)S(1)} %bitcast.176), channel_id=1, source_target_pairs={{0,1},{1,0},{2,3},{3,2},{4,5},{5,4},{6,7},{7,6},{8,9},{9,8},{10,11... | collective-permute-start | bytes 1179656 | tf_op jit(solution)/shard_map/cond/branch_1_fun/ppermute | solution.py:78
  12.7 3.4 %collective-permute-start.28 = (bf16[2,128,768]{2,1,0:T(8,128)(2,1)S(1)}, bf16[2,128,768]{2,1,0:T(8,128)(2,1)S(1)}, u32[]{:S(2)}, u32[]{:S(2)}) collective-permute-start(bf16[2,128,768]{2,1,0:T(8,128)(2,1)S(1)} %collective-permute-done.27.refs_2_), channel_id=1, source_target_pairs={{0,1},{1,0},{2,3},{3,2},{4,5},{5,4},{6,7},{7,6},{8,9},{9,8},{10,11... | collective-permute-start | bytes 1179656 | tf_op jit(solution)/shard_map/cond/branch_1_fun/ppermute | solution.py:78
  14.7 18.8 %collective-permute-start.29 = (bf16[1536,256]{1,0:T(8,128)(2,1)S(1)}, bf16[1536,256]{1,0:T(8,128)(2,1)S(1)}, u32[]{:S(2)}, u32[]{:S(2)}) collective-permute-start(bf16[1536,256]{1,0:T(8,128)(2,1)S(1)} %get-tuple-element.153.refs_0_.refs_4_.refs_2_.refs_6_), channel_id=1, source_target_pairs={{0,1},{1,0},{2,3},{3,2},{4,5},{5,4},{6,7},{7,6},{8,9},{9,8},{10,11... | collective-permute-start | bytes 2359304 | tf_op jit(solution)/shard_map/cond/branch_1_fun/ppermute | solution.py:78
  16.1 17.5 %copy-start.10 = (f32[1,1024,768]{2,1,0:T(8,128)S(1)}, f32[1,1024,768]{2,1,0:T(8,128)}, u32[]{:S(2)}) copy-start(f32[1,1024,768]{2,1,0:T(8,128)} %get-tuple-element.159) | copy-start | bytes 9437188 | tf_op jit(solution)/shard_map/cond
  29.5 4.0 %copy-start.4 = (bf16[1,1024,768]{2,1,0:T(8,128)(2,1)S(1)}, bf16[1,1024,768]{2,1,0:T(8,128)(2,1)}, u32[]{:S(2)}) copy-start(bf16[1,1024,768]{2,1,0:T(8,128)(2,1)} %get-tuple-element.157) | copy-start | bytes 4718596 | tf_op jit(solution)/shard_map/cond
  29.5 4.0 %copy-start.7 = (f32[1,1024,768]{2,1,0:T(8,128)S(1)}, f32[1,1024,768]{2,1,0:T(8,128)}, u32[]{:S(2)}) copy-start(f32[1,1024,768]{2,1,0:T(8,128)} %get-tuple-element.158) | copy-start | bytes 9437188 | tf_op jit(solution)/shard_map/cond
  29.5 4.0 %collective-permute-start.31 = (bf16[1536,256]{1,0:T(8,128)(2,1)S(1)}, bf16[1536,256]{1,0:T(8,128)(2,1)S(1)}, u32[]{:S(2)}, u32[]{:S(2)}) collective-permute-start(bf16[1536,256]{1,0:T(8,128)(2,1)S(1)} %collective-permute-done.30.refs_2_.refs_6_.refs_4_.refs_8_), channel_id=1, source_target_pairs={{0,1},{1,0},{2,3},{3,2},{4,5},{5,4},{6,7},{7,6},{8,9},{9,8},{10,11... | collective-permute-start | bytes 2359304 | tf_op jit(solution)/shard_map/cond/branch_1_fun/ppermute | solution.py:78
  30.8 11.6 %collective-permute-start.33 = (bf16[384,512]{1,0:T(8,128)(2,1)S(1)}, bf16[384,512]{1,0:T(8,128)(2,1)S(1)}, u32[]{:S(2)}, u32[]{:S(2)}) collective-permute-start(bf16[384,512]{1,0:T(8,128)(2,1)S(1)} %get-tuple-element.164), channel_id=1, source_target_pairs={{0,2},{1,3},{2,0},{3,1},{4,6},{5,7},{6,4},{7,5},{8,10},{9,11},{10,... | collective-permute-start | bytes 1179656 | tf_op jit(solution)/shard_map/cond/branch_1_fun/ppermute | solution.py:78
  32.4 17.9 %collective-permute-start.32 = (bf16[384,512]{1,0:T(8,128)(2,1)S(1)}, bf16[384,512]{1,0:T(8,128)(2,1)S(1)}, u32[]{:S(2)}, u32[]{:S(2)}) collective-permute-start(bf16[384,512]{1,0:T(8,128)(2,1)S(1)} %get-tuple-element.163.refs_0_.refs_10_), channel_id=1, source_target_pairs={{0,1},{1,0},{2,3},{3,2},{4,5},{5,4},{6,7},{7,6},{8,9},{9,8},{10,11... | collective-permute-start | bytes 1179656 | tf_op jit(solution)/shard_map/cond/branch_1_fun/ppermute | solution.py:78
  36.5 13.5 %collective-permute-start.35 = (bf16[256,768]{1,0:T(8,128)(2,1)S(1)}, bf16[256,768]{1,0:T(8,128)(2,1)S(1)}, u32[]{:S(2)}, u32[]{:S(2)}) collective-permute-start(bf16[256,768]{1,0:T(8,128)(2,1)S(1)} %get-tuple-element.173.refs_0_), channel_id=1, source_target_pairs={{0,8},{4,12},{8,0},{12,4},{16,24},{20,28},{24,16},{28,20},{1,9},{5... | collective-permute-start | bytes 1179656 | tf_op jit(solution)/shard_map/cond/branch_1_fun/ppermute | solution.py:117
  42.4 8.0 %collective-permute-start.34 = (bf16[384,512]{1,0:T(8,128)(2,1)S(1)}, bf16[384,512]{1,0:T(8,128)(2,1)S(1)}, u32[]{:S(2)}, u32[]{:S(2)}) collective-permute-start(bf16[384,512]{1,0:T(8,128)(2,1)S(1)} %collective-permute-done.33.refs_2_.refs_12_), channel_id=1, source_target_pairs={{0,1},{1,0},{2,3},{3,2},{4,5},{5,4},{6,7},{7,6},{8,9},{9,8},{10,11... | collective-permute-start | bytes 1179656 | tf_op jit(solution)/shard_map/cond/branch_1_fun/ppermute | solution.py:78
  43.0 18.1 %collective-permute-start.36 = (bf16[256,768]{1,0:T(8,128)(2,1)S(1)}, bf16[256,768]{1,0:T(8,128)(2,1)S(1)}, u32[]{:S(2)}, u32[]{:S(2)}) collective-permute-start(bf16[256,768]{1,0:T(8,128)(2,1)S(1)} %get-tuple-element.168.refs_2_), channel_id=1, source_target_pairs={{0,8},{4,12},{8,0},{12,4},{16,24},{20,28},{24,16},{28,20},{1,9},{5... | collective-permute-start | bytes 1179656 | tf_op jit(solution)/shard_map/cond/branch_1_fun/ppermute | solution.py:117
  48.5 11.6 %collective-permute-start.37 = (bf16[192,512]{1,0:T(8,128)(2,1)S(1)}, bf16[192,512]{1,0:T(8,128)(2,1)S(1)}, u32[]{:S(2)}, u32[]{:S(2)}) collective-permute-start(bf16[192,512]{1,0:T(8,128)(2,1)S(1)} %get-tuple-element.179), channel_id=1, source_target_pairs={{0,3},{1,2},{2,1},{3,0},{4,7},{5,6},{6,5},{7,4},{8,11},{9,10},{10,... | collective-permute-start | bytes 589832 | tf_op jit(solution)/shard_map/cond/branch_1_fun/ppermute | solution.py:78
  50.0 16.9 %collective-permute-start.41 = (bf16[192,512]{1,0:T(8,128)(2,1)S(1)}, bf16[192,512]{1,0:T(8,128)(2,1)S(1)}, u32[]{:S(2)}, u32[]{:S(2)}) collective-permute-start(bf16[192,512]{1,0:T(8,128)(2,1)S(1)} %get-tuple-element.185), channel_id=1, source_target_pairs={{0,1},{1,0},{2,3},{3,2},{4,5},{5,4},{6,7},{7,6},{8,9},{9,8},{10,11... | collective-permute-start | bytes 589832 | tf_op jit(solution)/shard_map/cond/branch_1_fun/ppermute | solution.py:78
  50.2 17.9 %collective-permute-start.42 = (bf16[192,512]{1,0:T(8,128)(2,1)S(1)}, bf16[192,512]{1,0:T(8,128)(2,1)S(1)}, u32[]{:S(2)}, u32[]{:S(2)}) collective-permute-start(bf16[192,512]{1,0:T(8,128)(2,1)S(1)} %get-tuple-element.186), channel_id=1, source_target_pairs={{0,2},{1,3},{2,0},{3,1},{4,6},{5,7},{6,4},{7,5},{8,10},{9,11},{10,... | collective-permute-start | bytes 589832 | tf_op jit(solution)/shard_map/cond/branch_1_fun/ppermute | solution.py:78
  59.5 6.2 %copy-start.13 = (f32[1024,768]{1,0:T(8,128)}, f32[1024,768]{1,0:T(8,128)S(1)}, u32[]{:S(2)}) copy-start(f32[1024,768]{1,0:T(8,128)S(1)} %get-tuple-element.206) | copy-start | bytes 9437188 | tf_op jit(solution)/shard_map/cond
  59.6 6.2 %copy-start.16 = (f32[1024,768]{1,0:T(8,128)}, f32[1024,768]{1,0:T(8,128)S(1)}, u32[]{:S(2)}) copy-start(f32[1024,768]{1,0:T(8,128)S(1)} %get-tuple-element.207) | copy-start | bytes 9437188 | tf_op jit(solution)/shard_map/cond
  59.6 18.5 %collective-permute-start.44 = (bf16[256,768]{1,0:T(8,128)(2,1)S(1)}, bf16[256,768]{1,0:T(8,128)(2,1)S(1)}, u32[]{:S(2)}, u32[]{:S(2)}) collective-permute-start(bf16[256,768]{1,0:T(8,128)(2,1)S(1)} %get-tuple-element.190.refs_6_), channel_id=1, source_target_pairs={{0,8},{4,12},{8,0},{12,4},{16,24},{20,28},{24,16},{28,20},{1,9},{5... | collective-permute-start | bytes 1179656 | tf_op jit(solution)/shard_map/cond/branch_1_fun/ppermute | solution.py:117
  60.2 18.0 %collective-permute-start.43 = (bf16[256,768]{1,0:T(8,128)(2,1)S(1)}, bf16[256,768]{1,0:T(8,128)(2,1)S(1)}, u32[]{:S(2)}, u32[]{:S(2)}) collective-permute-start(bf16[256,768]{1,0:T(8,128)(2,1)S(1)} %get-tuple-element.189.refs_4_), channel_id=1, source_target_pairs={{0,8},{4,12},{8,0},{12,4},{16,24},{20,28},{24,16},{28,20},{1,9},{5... | collective-permute-start | bytes 1179656 | tf_op jit(solution)/shard_map/cond/branch_1_fun/ppermute | solution.py:117
  61.1 7.5 %copy-start.19 = (f32[1,192,4096]{2,1,0:T(8,128)S(1)}, f32[1,192,4096]{2,1,0:T(8,128)}, u32[]{:S(2)}) copy-start(f32[1,192,4096]{2,1,0:T(8,128)} %get-tuple-element.145) | copy-start | bytes 9437188 | tf_op jit(solution)/shard_map/cond
  61.1 7.5 %copy-start.22 = (f32[1,192,4096]{2,1,0:T(8,128)S(1)}, f32[1,192,4096]{2,1,0:T(8,128)}, u32[]{:S(2)}) copy-start(f32[1,192,4096]{2,1,0:T(8,128)} %get-tuple-element.146) | copy-start | bytes 9437188 | tf_op jit(solution)/shard_map/cond
  65.7 5.9 %collective-permute-start.38 = (bf16[192,512]{1,0:T(8,128)(2,1)S(1)}, bf16[192,512]{1,0:T(8,128)(2,1)S(1)}, u32[]{:S(2)}, u32[]{:S(2)}) collective-permute-start(bf16[192,512]{1,0:T(8,128)(2,1)S(1)} %get-tuple-element.181), channel_id=1, source_target_pairs={{0,1},{1,0},{2,3},{3,2},{4,5},{5,4},{6,7},{7,6},{8,9},{9,8},{10,11... | collective-permute-start | bytes 589832 | tf_op jit(solution)/shard_map/cond/branch_1_fun/ppermute | solution.py:78
  66.9 8.3 %collective-permute-start.39 = (bf16[192,512]{1,0:T(8,128)(2,1)S(1)}, bf16[192,512]{1,0:T(8,128)(2,1)S(1)}, u32[]{:S(2)}, u32[]{:S(2)}) collective-permute-start(bf16[192,512]{1,0:T(8,128)(2,1)S(1)} %get-tuple-element.182), channel_id=1, source_target_pairs={{0,2},{1,3},{2,0},{3,1},{4,6},{5,7},{6,4},{7,5},{8,10},{9,11},{10,... | collective-permute-start | bytes 589832 | tf_op jit(solution)/shard_map/cond/branch_1_fun/ppermute | solution.py:78
  68.2 9.9 %collective-permute-start.40 = (bf16[192,512]{1,0:T(8,128)(2,1)S(1)}, bf16[192,512]{1,0:T(8,128)(2,1)S(1)}, u32[]{:S(2)}, u32[]{:S(2)}) collective-permute-start(bf16[192,512]{1,0:T(8,128)(2,1)S(1)} %get-tuple-element.183), channel_id=1, source_target_pairs={{0,3},{1,2},{2,1},{3,0},{4,7},{5,6},{6,5},{7,4},{8,11},{9,10},{10,... | collective-permute-start | bytes 589832 | tf_op jit(solution)/shard_map/cond/branch_1_fun/ppermute | solution.py:78
  71.6 32.5 %collective-permute-start.46 = (bf16[4,192,512]{2,1,0:T(8,128)(2,1)S(1)}, bf16[4,192,512]{2,1,0:T(8,128)(2,1)S(1)}, u32[]{:S(2)}, u32[]{:S(2)}) collective-permute-start(bf16[4,192,512]{2,1,0:T(8,128)(2,1)S(1)} %get-tuple-element.192.refs_14_.own_ref), channel_id=1, source_target_pairs={{0,8},{4,12},{8,0},{12,4},{16,24},{20,28},{24,16},{28,20},{1,9},{5... | collective-permute-start | bytes 2359304 | tf_op jit(solution)/shard_map/cond/branch_1_fun/ppermute | solution.py:117
  81.1 29.4 %copy-start.25 = (f32[192,4096]{1,0:T(8,128)}, f32[192,4096]{1,0:T(8,128)S(1)}, u32[]{:S(2)}) copy-start(f32[192,4096]{1,0:T(8,128)S(1)} %get-tuple-element.204) | copy-start | bytes 9437188 | tf_op jit(solution)/shard_map/cond
  81.1 29.4 %copy-start.28 = (f32[192,4096]{1,0:T(8,128)}, f32[192,4096]{1,0:T(8,128)S(1)}, u32[]{:S(2)}) copy-start(f32[192,4096]{1,0:T(8,128)S(1)} %get-tuple-element.205) | copy-start | bytes 9437188 | tf_op jit(solution)/shard_map/cond
  81.1 34.8 %collective-permute-start.45 = (bf16[4,192,512]{2,1,0:T(8,128)(2,1)S(1)}, bf16[4,192,512]{2,1,0:T(8,128)(2,1)S(1)}, u32[]{:S(2)}, u32[]{:S(2)}) collective-permute-start(bf16[4,192,512]{2,1,0:T(8,128)(2,1)S(1)} %get-tuple-element.194.own_ref), channel_id=1, source_target_pairs={{0,8},{4,12},{8,0},{12,4},{16,24},{20,28},{24,16},{28,20},{1,9},{5... | collective-permute-start | bytes 2359304 | tf_op jit(solution)/shard_map/cond/branch_1_fun/ppermute | solution.py:117
  81.7 4.5 %collective-permute-start.47 = (bf16[256,768]{1,0:T(8,128)(2,1)S(1)}, bf16[256,768]{1,0:T(8,128)(2,1)S(1)}, u32[]{:S(2)}, u32[]{:S(2)}) collective-permute-start(bf16[256,768]{1,0:T(8,128)(2,1)S(1)} %get-tuple-element.197), channel_id=1, source_target_pairs={{0,1},{1,0},{2,3},{3,2},{4,5},{5,4},{6,7},{7,6},{8,9},{9,8},{10,11... | collective-permute-start | bytes 1179656 | tf_op jit(solution)/shard_map/cond/branch_1_fun/ppermute | solution.py:78
  84.5 10.7 %collective-permute-start.48 = (bf16[256,768]{1,0:T(8,128)(2,1)S(1)}, bf16[256,768]{1,0:T(8,128)(2,1)S(1)}, u32[]{:S(2)}, u32[]{:S(2)}) collective-permute-start(bf16[256,768]{1,0:T(8,128)(2,1)S(1)} %get-tuple-element.198), channel_id=1, source_target_pairs={{0,2},{1,3},{2,0},{3,1},{4,6},{5,7},{6,4},{7,5},{8,10},{9,11},{10,... | collective-permute-start | bytes 1179656 | tf_op jit(solution)/shard_map/cond/branch_1_fun/ppermute | solution.py:78
  85.4 18.7 %collective-permute-start.49 = (bf16[256,768]{1,0:T(8,128)(2,1)S(1)}, bf16[256,768]{1,0:T(8,128)(2,1)S(1)}, u32[]{:S(2)}, u32[]{:S(2)}) collective-permute-start(bf16[256,768]{1,0:T(8,128)(2,1)S(1)} %get-tuple-element.199), channel_id=1, source_target_pairs={{0,3},{1,2},{2,1},{3,0},{4,7},{5,6},{6,5},{7,4},{8,11},{9,10},{10,... | collective-permute-start | bytes 1179656 | tf_op jit(solution)/shard_map/cond/branch_1_fun/ppermute | solution.py:78
  105.3 5.2 %collective-permute-start.50 = (bf16[2,8,768]{2,1,0:T(8,128)(2,1)S(1)}, bf16[2,8,768]{2,1,0:T(8,128)(2,1)S(1)}, u32[]{:S(2)}, u32[]{:S(2)}) collective-permute-start(bf16[2,8,768]{2,1,0:T(8,128)(2,1)S(1)} %get-tuple-element.201), channel_id=1, source_target_pairs={{0,1},{1,2},{2,3},{4,5},{5,6},{6,7},{8,9},{9,10},{10,11},{12,13},{... | collective-permute-start | bytes 73736 | tf_op jit(solution)/shard_map/cond/branch_1_fun/ppermute | solution.py:845
  107.9 5.1 %collective-permute-start.51 = (bf16[2,8,768]{2,1,0:T(8,128)(2,1)S(1)}, bf16[2,8,768]{2,1,0:T(8,128)(2,1)S(1)}, u32[]{:S(2)}, u32[]{:S(2)}) collective-permute-start(bf16[2,8,768]{2,1,0:T(8,128)(2,1)S(1)} %get-tuple-element.202), channel_id=1, source_target_pairs={{1,0},{2,1},{3,2},{5,4},{6,5},{7,6},{9,8},{10,9},{11,10},{13,12},{... | collective-permute-start | bytes 73736 | tf_op jit(solution)/shard_map/cond/branch_1_fun/ppermute | solution.py:846
  110.5 5.5 %copy-start.31 = (bf16[1024,768]{1,0:T(8,128)(2,1)}, bf16[1024,768]{1,0:T(8,128)(2,1)S(1)}, u32[]{:S(2)}) copy-start(bf16[1024,768]{1,0:T(8,128)(2,1)S(1)} %mean_project.4.refs_1_) | copy-start | bytes 4718596 | tf_op jit(solution)/shard_map/cond
  114.3 3.3 %copy-start.34 = (bf16[2,128,768]{2,1,0:T(8,128)(2,1)}, bf16[2,128,768]{2,1,0:T(8,128)(2,1)S(1)}, u32[]{:S(2)}) copy-start(bf16[2,128,768]{2,1,0:T(8,128)(2,1)S(1)} %conv_back.4.refs_0_) | copy-start | bytes 1179652 | tf_op jit(solution)/shard_map/cond
where the time goes:
time: 118 us
  Pallas kernels  48.6 us (41%)
  waiting for transfers between devices  36.8 us (31%)
  starting transfers between devices  27.8 us (24%)
  loops' own time  1.37 us (1%)
  between operations  1.34 us (1%)
    ppermute x18, waiting for transfers between devices, xor_perm(): return lax.ppermute(value, 'fsdp', [(i, i ^ off) for i in range(count)])  34.1 us
    ppermute x18, starting transfers between devices, xor_perm(): return lax.ppermute(value, 'fsdp', [(i, i ^ off) for i in range(count)])  18.2 us
    pallas_call x4, Pallas kernels, hidden_chunk(): pl.pallas_call(partial(hidden_kernel, count=count, first=grads is None),...  16.5 us
    pallas_call x2, Pallas kernels, expand_chunk(): pl.pallas_call(partial(expand_kernel, count=count), out_shape=[jax.ShapeD...  9.15 us
    pallas_call x1, Pallas kernels, norm_rows(): pl.pallas_call(partial(norm_kernel, count=count, tile=math.gcd(steps, 128...  6.12 us
    pallas_call x2, Pallas kernels, update_chunk(): pl.pallas_call(partial(update_kernel, count=count), out_shape=[jax.ShapeD...  5.89 us
    ppermute x6, starting transfers between devices, swap_gossip(): lax.ppermute(value, 'gossip', [(i, i ^ 1 << level) for i in range(count)])  5.07 us
    pallas_call x2, Pallas kernels, mean_expand(): pl.pallas_call(mean_expand_kernel, out_shape=pltpu.HBM((rows, full), BF16...  3.23 us
  transfers between devices with their start and end apart: 26, of which 8 were waited for; matrix products, arithmetic and copies ran while one was open for 1% of the time, Pallas kernels for 40%

commit v1 on v0

--- a/solution.py
+++ b/solution.py
@@ -18,6 +18,7 @@
 INV_ROOT_TAU = 0.3989422804014327
 PAD = 8
 BLOCK = 256
+EXPAND_UNROLL = False
 F32 = jnp.float32
 BF16 = jnp.bfloat16
 MIB = 1 << 20
@@ -68,7 +69,7 @@
 def plan(owned):
     if owned % 1024 == 0:
         q = owned // 4
-        return ranges([2 * q, 2 * q]), ranges([q] * 4), ranges([2 * q, 2 * q])
+        return ranges([2 * q, 2 * q]), ranges([q, q, 2 * q]), ranges([2 * q, 2 * q])
     half = owned // 2
     return ranges([owned]), ranges([half, half]), ranges([owned])
 
@@ -121,17 +122,17 @@
     refs[-1][...] = jnp.zeros(refs[-1].shape, F32)
 
 
-def token(value, name):
+def token(values, name):
     shape = jax.ShapeDtypeStruct((8, 128), F32)
     return pl.pallas_call(
         token_kernel,
         out_shape=shape,
-        in_specs=[hbm()],
+        in_specs=[hbm()] * len(values),
         out_specs=pl.BlockSpec(memory_space=pltpu.VMEM),
         compiler_params=params(MIB),
         cost_estimate=cost(40 * MIB),
         name=name,
-    )(value)
+    )(*values)
 
 
 def slice_kernel(me_ref, *refs, count):
@@ -177,12 +178,20 @@
     rows, width = cot_ref.shape
     part, size = blocks[0].shape
     panels = width // size
-    masked = (cot_ref[...].astype(F32) * seen_ref[...]).astype(BF16)
-    masked_ref[...] = masked
-    branch = (masked.astype(F32) * scale_ref[...]).astype(BF16)
-    for out in outs:
-        for p in range(panels):
-            out[p * rows : (p + 1) * rows] = branch[:, p * size : (p + 1) * size]
+    tile = 64
+
+    def body(i, carry):
+        here = pl.ds(pl.multiple_of(i * tile, tile), tile)
+        masked = (cot_ref[here].astype(F32) * seen_ref[here]).astype(BF16)
+        masked_ref[here] = masked
+        branch = (masked.astype(F32) * scale_ref[...]).astype(BF16)
+        for out in outs:
+            for p in range(panels):
+                there = pl.ds(pl.multiple_of(p * rows + i * tile, tile), tile)
+                out[there] = branch[:, p * size : (p + 1) * size]
+        return carry
+
+    lax.fori_loop(0, rows // tile, body, 0)
     for off in range(count):
         for k in range(spans):
             low = panels * rows + (off % 2 * spans + k) * part
@@ -261,7 +270,7 @@
     rows = seqs * steps
     total = count * rows
     return pl.pallas_call(
-        partial(norm_kernel, count=count, tile=math.gcd(steps, 128)),
+        partial(norm_kernel, count=count, tile=math.gcd(steps, 64)),
         out_shape=[
             jax.ShapeDtypeStruct((total, width), BF16),
             jax.ShapeDtypeStruct((width, total), BF16),
@@ -318,14 +327,17 @@
         joined[pl.ds(start, part), columns] = piece[...]
 
 
-def hidden_kernel(me_ref, corr_ref, normed_ref, w_ref, m_ref, v_ref, *refs, count, first):
+def hidden_kernel(
+    me_ref, corr_ref, normed_ref, w_ref, m_ref, v_ref, *refs, count, first, splits
+):
     wide = refs[:count]
     if first:
         packs = refs[count : 2 * count]
-        updated_ref, first_ref, second_ref, slope_ref, grads_ref, joined, total = refs[-7:]
+        *outs, first_ref, second_ref, slope_ref, grads_ref = refs[-splits - 7 : -3]
     else:
         grads_ref = refs[count]
-        updated_ref, first_ref, second_ref, slope_ref, joined, total = refs[-6:]
+        *outs, first_ref, second_ref, slope_ref = refs[-splits - 6 : -3]
+    joined, total, updated = refs[-3:]
     join_rows(me_ref[0], wide, joined)
     width = normed_ref.shape[1]
     rows = normed_ref.shape[0] // count
@@ -348,18 +360,23 @@
         slope_ref[part] = (cumul + pre * density).astype(BF16)
         total[...] += dot(hidden, grads_ref[part], (0, 0))
 
-    loop(count, body, first)
+    loop(count, body, True)
     adam_tiles(
         w_ref,
         m_ref,
         v_ref,
         lambda rows: total[rows] * corr_ref[2],
         corr_ref,
-        updated_ref,
+        updated if splits > 1 else outs[0],
         first_ref,
         second_ref,
         32,
     )
+    for k in range(splits if splits > 1 else 0):
+
+        @pl.when(pl.program_id(0) == k)
+        def _():
+            outs[k][...] = updated[...]
 
 
 def hidden_chunk(me, corr, span, normed, grads, w, m, v, wide, low, previous, after):
@@ -369,6 +386,7 @@
     start, size = span
     block = min(BLOCK, size)
     base = start // block
+    splits = size // block
     rows = total // count
     row_block = pl.BlockSpec((block, width), lambda f, *_: (base + f, 0))
     arrays = [array for array, _ in wide]
@@ -388,9 +406,9 @@
     chained = previous is not None
     last = 6 + count + len(extra)
     return pl.pallas_call(
-        partial(hidden_kernel, count=count, first=grads is None),
-        out_shape=[
-            jax.ShapeDtypeStruct((size, width), BF16),
+        partial(hidden_kernel, count=count, first=grads is None, splits=splits),
+        out_shape=[jax.ShapeDtypeStruct((block, width), BF16)] * splits
+        + [
             jax.ShapeDtypeStruct(m.shape, F32),
             jax.ShapeDtypeStruct(v.shape, F32),
             jax.ShapeDtypeStruct((total, owned), BF16),
@@ -398,22 +416,28 @@
         + out_grads,
         grid_spec=pltpu.PrefetchScalarGridSpec(
             num_scalar_prefetch=2,
-            grid=(size // block,),
+            grid=(splits,),
             in_specs=[whole(normed), row_block, row_block, row_block]
             + wide_specs
             + more
             + ([hbm()] * 3 if chained else [])
             + [hbm()] * len(after),
-            out_specs=[
-                pl.BlockSpec((block, width), lambda f, *_: (f, 0)),
+            out_specs=[pl.BlockSpec((block, width), lambda f, *_: (0, 0))] * splits
+            + [
                 row_block,
                 row_block,
                 pl.BlockSpec((total, block), lambda f, *_: (0, base + f)),
             ]
             + [whole(g) for g in out_grads],
-            scratch_shapes=[pltpu.VMEM((width, block), BF16), pltpu.VMEM((block, width), F32)],
+            scratch_shapes=[
+                pltpu.VMEM((width, block), BF16),
+                pltpu.VMEM((block, width), F32),
+                pltpu.VMEM((block, width), BF16),
+            ],
         ),
-        input_output_aliases={last: 1, last + 1: 2, last + 2: 3} if chained else {},
+        input_output_aliases=(
+            {last + j: splits + j for j in range(3)} if chained else {}
+        ),
         compiler_params=params(20 * MIB + 5 * total * width * 2),
         cost_estimate=cost(),
         name=f"hidden_{start}",
@@ -431,7 +455,7 @@
         back = dot(grads_ref[part], w_ref[...], (1, 1)) * corr_ref[2]
         pre_ref[part] = (back * slope_ref[part].astype(F32)).astype(BF16)
 
-    loop(count, body)
+    loop(count, body, EXPAND_UNROLL)
     scratch[...] = (dot(turned_ref[...], pre_ref[...]) * scale_in).astype(BF16)
     piece = width // count
     for off in range(count):
@@ -469,9 +493,9 @@
     )(me, corr, turned, grads, w, slope, *after)
 
 
-def update_kernel(me_ref, corr_ref, w_ref, m_ref, v_ref, *refs, count):
+def update_kernel(me_ref, corr_ref, w_ref, m_ref, v_ref, *refs, count, splits):
     pieces = refs[:count]
-    updated_ref, first_ref, second_ref, held = refs[-4:]
+    *outs, first_ref, second_ref, held, updated = refs[-splits - 4 :]
     for off in range(count):
 
         @pl.when(pl.program_id(0) == off)
@@ -484,15 +508,21 @@
         v_ref,
         lambda rows: held[rows].astype(F32),
         corr_ref,
-        updated_ref.at[0],
+        updated,
         first_ref,
         second_ref,
         48,
     )
-
-
-def update_chunk(me, corr, span, w, m, v, pieces, previous, after):
+    for h in range(splits):
+
+        @pl.when(pl.program_id(0) // (count // splits) == h)
+        def _():
+            outs[h][0] = updated[...]
+
+
+def update_chunk(me, corr, span, w, m, v, pieces, splits, previous, after):
     count = len(pieces)
+    half = count // splits
     rows, size = pieces[0].shape
     start, _ = span
     ratio = w.shape[1] // count // size
@@ -501,12 +531,9 @@
     chained = previous is not None
     last = 5 + count
     return pl.pallas_call(
-        partial(update_kernel, count=count),
-        out_shape=[
-            jax.ShapeDtypeStruct((count, rows, size), BF16),
-            jax.ShapeDtypeStruct(m.shape, F32),
-            jax.ShapeDtypeStruct(v.shape, F32),
-        ],
+        partial(update_kernel, count=count, splits=splits),
+        out_shape=[jax.ShapeDtypeStruct((half, rows, size), BF16)] * splits
+        + [jax.ShapeDtypeStruct(m.shape, F32), jax.ShapeDtypeStruct(v.shape, F32)],
         grid_spec=pltpu.PrefetchScalarGridSpec(
             num_scalar_prefetch=2,
             grid=(count,),
@@ -515,13 +542,16 @@
             + ([hbm()] * 2 if chained else [])
             + [hbm()] * len(after),
             out_specs=[
-                pl.BlockSpec((1, rows, size), lambda i, *_: (i, 0, 0)),
-                column,
-                column,
-            ],
-            scratch_shapes=[pltpu.VMEM((rows, size), BF16)],
+                pl.BlockSpec(
+                    (1, rows, size),
+                    lambda i, *_, h=h: (jnp.clip(i - h * half, 0, half - 1).astype(jnp.int32), 0, 0),
+                )
+                for h in range(splits)
+            ]
+            + [column, column],
+            scratch_shapes=[pltpu.VMEM((rows, size), BF16)] * 2,
         ),
-        input_output_aliases={last: 1, last + 1: 2} if chained else {},
+        input_output_aliases={last: splits, last + 1: splits + 1} if chained else {},
         compiler_params=params(24 * MIB),
         cost_estimate=cost(),
         name=f"update_{start}",
@@ -566,9 +596,9 @@
     mean_tiles(own_ref.at[0], other_ref.at[0], refs[-1])
 
 
-def mean_expand(me, span, own, other, full, previous, after):
+def mean_expand(me, span, lead, own, other, full, owned, previous, after):
     count, rows, size = own.shape
-    ratio = full // count // size
+    ratio = owned // size
     base = span[0] // size
     in_spec = pl.BlockSpec((1, rows, size), lambda i, m: (i, 0, 0))
     chained = previous is not None
@@ -579,12 +609,12 @@
             num_scalar_prefetch=1,
             grid=(count,),
             in_specs=[in_spec, in_spec] + [hbm()] * (chained + len(after)),
-            out_specs=pl.BlockSpec((rows, size), lambda i, m: (0, (m[0] ^ i) * ratio + base)),
+            out_specs=pl.BlockSpec((rows, size), lambda i, m: (0, (m[0] ^ (i + lead)) * ratio + base)),
         ),
         input_output_aliases={3: 0} if chained else {},
         compiler_params=params(16 * MIB),
         cost_estimate=cost(),
-        name=f"mean_expand_{span[0]}",
+        name=f"mean_expand_{span[0]}_{lead}",
     )(me, own, other, *((previous,) if chained else ()), *after)
 
 
@@ -797,19 +827,21 @@
         if i == 0:
             after = ()
         elif i == 2:
-            after = (token(project_pairs[0][1], "first_arrived"), *pre)
+            after = (token([project_pairs[0][1]], "first_arrived"), *pre)
         else:
             after = ()
         at = max(j for j, (low, _) in enumerate(spans) if low <= start)
         low = start - spans[at][0]
-        updated, *carried = hidden_chunk(
+        outs = hidden_chunk(
             me, corr, (start, size), normed, grads, wp, mp_ax, vp_ax, wide[at], low, carried, after
         )
+        splits = max(1, size // BLOCK)
+        updates, carried = outs[:splits], list(outs[splits:])
         if i == 0:
             grads = carried.pop()
         if i == 1:
-            wide += [pieces_of(relay_packs(packs, (updated,)), 0, 1, 0) for packs in received]
-        project_pairs.append((updated, swap_gossip(updated, level)))
+            wide += [pieces_of(relay_packs(packs, (updates[0],)), 0, 1, 0) for packs in received]
+        project_pairs += [(updated, swap_gossip(updated, level)) for updated in updates]
         done = start + size
         while pending and sum(pending[0]) <= done:
             after = (project_pairs[1][1], expand_pairs[0][-1]) if len(pre) else ()
@@ -824,19 +856,34 @@
     for i, span in enumerate(groups):
         last = i + 1 == len(groups)
         if last:
-            back = row_grads(me, pre, wide, spans, width, tuple(u for u, _ in expand_pairs[:i]))
-            after = (*(other for _, other in project_pairs[2:]), back[0])
+            done = tuple(pairs[0][0] for pairs in expand_pairs[:i])
+            back = row_grads(me, pre, wide, spans, width, done)
+            after = (project_pairs[-1][1], back[0])
         else:
-            after = ()
-        updated, *moments = update_chunk(
-            me, corr, span, we, me_ax, ve_ax, expand_pairs[i], moments, after
+            after = (project_pairs[2][1],)
+        splits = 2 if last else 1
+        last_blocks = expand_pairs[i][1:]
+        outs = update_chunk(
+            me, corr, span, we, me_ax, ve_ax, expand_pairs[i], splits, moments, after
         )
-        expand_pairs[i] = (updated, swap_gossip(updated, level))
+        moments = outs[splits:]
+        expand_pairs[i] = [(updated, swap_gossip(updated, level)) for updated in outs[:splits]]
     first_expand_next, second_expand_next = moments
 
+    back = list(back)
+    back[1] = lax.optimization_barrier((back[1], expand_pairs[-1][-1][0]))[0]
+    back[2:] = lax.optimization_barrier((*back[2:], *last_blocks))[: count - 2]
     back_pieces = swap_blocks(back)
 
-    after = tuple(other for _, other in expand_pairs[:-1])
+    shared_project = mean_project(project_pairs, ranges([p[0].shape[0] for p in project_pairs]))
+    shared_expand = None
+    for span, pairs in zip(groups[:-1], expand_pairs):
+        for own, other in pairs:
+            shared_expand = mean_expand(
+                me, span, 0, own, other, hidden_width, owned, shared_expand, ()
+            )
+    lead = 0
+    after = (shared_project,) if shared_expand is None else (shared_project, shared_expand)
     grad_conv, first_rows, last_rows = norm_back(
         gain, unit, inv, back_pieces, seqs, steps, after
     )
@@ -846,11 +893,11 @@
     high = lax.ppermute(first_rows, "fsdp", backward)
     input_grad = conv_back(depth_kernel, grad_conv, low, high, masked, seqs)
 
-    shared_project = mean_project(project_pairs, parts)
-    shared_expand = None
-    for span, pair in zip(groups, expand_pairs):
-        after = (input_grad, shared_project) if shared_expand is None else ()
-        shared_expand = mean_expand(me, span, *pair, hidden_width, shared_expand, after)
+    for own, other in expand_pairs[-1]:
+        shared_expand = mean_expand(
+            me, groups[-1], lead, own, other, hidden_width, owned, shared_expand, (input_grad,)
+        )
+        lead += own.shape[0]
     return (
         shared_expand[None],
         shared_project[None],

time: 118 us -> 151 us (1.28)
  waiting for transfers between devices: 36.8 us -> 70.3 us
    ppermute x6 -> x7, waiting for transfers between devices: 0.09 us -> 25.8 us  [swap_gossip(): lax.ppermute(value, 'gossip', [(i, i ^ 1 << level) for i in range(count)])]
    ppermute x18, waiting for transfers between devices: 34.1 us -> 41.2 us  [xor_perm(): return lax.ppermute(value, 'fsdp', [(i, i ^ off) for i in range(count)])]
    pallas_call x8 -> x7, Pallas kernels: 28.5 us -> 27.5 us  [the longest x3 11.4 us: hidden_chunk(): pl.pallas_call(partial(hidden_kernel, count=count, first=grads is None, s...]
    ppermute x6 -> x7, starting transfers between devices: 5.07 us -> 5.81 us  [swap_gossip(): lax.ppermute(value, 'gossip', [(i, i ^ 1 << level) for i in range(count)])]
    pallas_call x2 -> x3, Pallas kernels: 3.23 us -> 3.56 us  [mean_expand(): pl.pallas_call(mean_expand_kernel, out_shape=pltpu.HBM((rows, full), BF16...]
  transfers between devices with their start and end apart: 26 -> 27, of which waited for: 8 -> 13; matrix products, arithmetic and copies ran while one was open for 1% -> 1% of each run, Pallas kernels for 40% -> 24%
where the time goes in v1:
time: 151 us
  waiting for transfers between devices  70.3 us (47%)
  Pallas kernels  48 us (32%)
  starting transfers between devices  28.2 us (19%)
    ppermute x18, waiting for transfers between devices, xor_perm(): return lax.ppermute(value, 'fsdp', [(i, i ^ off) for i in range(count)])  41.2 us
    ppermute x7, waiting for transfers between devices, swap_gossip(): lax.ppermute(value, 'gossip', [(i, i ^ 1 << level) for i in range(count)])  25.8 us
    ppermute x18, starting transfers between devices, xor_perm(): return lax.ppermute(value, 'fsdp', [(i, i ^ off) for i in range(count)])  17.5 us
    pallas_call x3, Pallas kernels, hidden_chunk(): pl.pallas_call(partial(hidden_kernel, count=count, first=grads is None, s...  11.4 us
    pallas_call x2, Pallas kernels, expand_chunk(): pl.pallas_call(partial(expand_kernel, count=count), out_shape=[jax.ShapeD...  9.11 us
    pallas_call x2, Pallas kernels, update_chunk(): pl.pallas_call(partial(update_kernel, count=count, splits=splits), out_sh...  8.32 us
    pallas_call x1, Pallas kernels, norm_rows(): pl.pallas_call(partial(norm_kernel, count=count, tile=math.gcd(steps, 64)...  7.74 us
    ppermute x7, starting transfers between devices, swap_gossip(): lax.ppermute(value, 'gossip', [(i, i ^ 1 << level) for i in range(count)])  5.81 us
  transfers between devices with their start and end apart: 27, of which 13 were waited for; matrix products, arithmetic and copies ran while one was open for 1% of the time, Pallas kernels for 24%

profile of v1, /device:TPU:1, one launch (start us, length us, event | category | flops | bytes accessed | tf_op | source)
XLA Modules:
  0.0 150.6 jit_solution(14273492239126841949)
XLA Ops:
  1.3 149.3 %conditional.1 = (bf16[1,192,4096]{2,1,0:T(8,128)(2,1)}, bf16[1,1024,768]{2,1,0:T(8,128)(2,1)}, f32[1,192,4096]{2,1,0:T(8,128)}, f32[1,192,4096]{2,1,0:T(8,128)}...) conditional(s32[]{:T(128)} %clamp.3, (s32[1]{0:T(128)}, ...), branch_computations={%region_0.1_spmd, %region_1.2_spmd, %region_2.3_spmd} | conditional | flops 288 | bytes 272942720 | solution.py:915
  1.3 2.1 %collective-permute-start.1 = (bf16[2,128,768]{2,1,0:T(8,128)(2,1)}, bf16[2,128,768]{2,1,0:T(8,128)(2,1)S(1)}, u32[]{:S(2)}, u32[]{:S(2)}) collective-permute-start(bf16[2,128,768]{2,1,0:T(8,128)(2,1)} %bitcast.163), channel_id=1, source_target_pairs={{0,2},{1,3},{2,0},{3,1},{4,6},{5,7},{6,4},{7,5},{8,10},{9,11},{10,... | collective-permute-start | bytes 1179656 | tf_op jit(solution)/shard_map/cond/branch_0_fun/ppermute | solution.py:79
  3.4 0.7 convert_element_type.19
  4.1 0.7 reshape.108.scale_ref
  4.8 0.1 copy.71.seen_ref
  5.0 0.0 copy-start.42
  5.0 0.0 copy-start.48
  5.0 1.9 %pack_first.3 = (bf16[1536,256]{1,0:T(8,128)(2,1)S(1)}, bf16[1536,256]{1,0:T(8,128)(2,1)S(1)}, bf16[256,768]{1,0:T(8,128)(2,1)S(1)}) custom-call(s32[1]{0:T(128)} %bitcast.me_ref, bf16[256,768]{1,0:T(8,128)(2,1)} %bitcast.160, f32[256,1]{1,0:T(8,128)S(1)} %copy.71.seen_ref, f32[1,768]{1,0:T(1,128)S(1)} %reshape.108.scale_ref, bf16[192,4096]{1,0:T(8,128)(2,1)} %bitcast.52, ...), custom_call_target="tpu_custom_call" | custom-call | flops 1 | bytes 1 | tf_op jit(solution)/shard_map/cond/branch_0_fun/pack_first/pallas_call | solution.py:206
  6.9 0.1 collective-permute-start.4
  7.0 1.0 collective-permute-start
  8.0 4.5 %collective-permute-done.1.refs_2_ = bf16[2,128,768]{2,1,0:T(8,128)(2,1)S(1)} collective-permute-done((bf16[2,128,768]{2,1,0:T(8,128)(2,1)}, bf16[2,128,768]{2,1,0:T(8,128)(2,1)S(1)}, u32[]{:S(2)}, u32[]{:S(2)}) %collective-permute-start.1) | collective-permute-done | bytes 393248 | tf_op jit(solution)/shard_map/cond/branch_0_fun/ppermute | solution.py:79
  12.5 2.1 %collective-permute-start.2 = (bf16[2,128,768]{2,1,0:T(8,128)(2,1)S(1)}, bf16[2,128,768]{2,1,0:T(8,128)(2,1)S(1)}, u32[]{:S(2)}, u32[]{:S(2)}) collective-permute-start(bf16[2,128,768]{2,1,0:T(8,128)(2,1)S(1)} %collective-permute-done.1.refs_2_), channel_id=1, source_target_pairs={{0,1},{1,0},{2,3},{3,2},{4,5},{5,4},{6,7},{7,6},{8,9},{9,8},{10,11... | collective-permute-start | bytes 1179656 | tf_op jit(solution)/shard_map/cond/branch_0_fun/ppermute | solution.py:79
  14.6 1.3 collective-permute-done.2.refs_3_
  15.9 7.7 %norm_rows.3 = (bf16[1024,768]{1,0:T(8,128)(2,1)S(1)}, bf16[768,1024]{1,0:T(8,128)(2,1)S(1)}, f32[256,768]{1,0:T(8,128)S(1)}, f32[256,128]{1,0:T(8,128)S(1)}) custom-call(s32[1]{0:T(128)} %bitcast.me_ref, f32[7,768]{1,0:T(8,128)S(1)} %copy-done.45, f32[1,768]{1,0:T(1,128)S(1)} %reshape.107.gain_ref, bf16[2,128,768]{2,1,0:T(8,128)(2,1)S(1)} %bitcast.165, ...), custom_call_target="tpu_custom_call" | custom-call | flops 1 | bytes 41943040 | tf_op jit(solution)/shard_map/cond/branch_0_fun/norm_rows/pallas_call | solution.py:272
  23.7 5.7 %collective-permute-done.4.refs_2_.refs_6_.refs_4_.refs_8_ = bf16[1536,256]{1,0:T(8,128)(2,1)S(1)} collective-permute-done((bf16[1536,256]{1,0:T(8,128)(2,1)S(1)}, bf16[1536,256]{1,0:T(8,128)(2,1)S(1)}, u32[]{:S(2)}, u32[]{:S(2)}) %collective-permute-start.4) | collective-permute-done | bytes 786464 | tf_op jit(solution)/shard_map/cond/branch_0_fun/ppermute | solution.py:79
  29.4 1.2 collective-permute-start.5
  30.6 0.1 slice_512.3
  30.6 1.5 %collective-permute-start.7 = (bf16[384,512]{1,0:T(8,128)(2,1)S(1)}, bf16[384,512]{1,0:T(8,128)(2,1)S(1)}, u32[]{:S(2)}, u32[]{:S(2)}) collective-permute-start(bf16[384,512]{1,0:T(8,128)(2,1)S(1)} %get-tuple-element.99), channel_id=1, source_target_pairs={{0,2},{1,3},{2,0},{3,1},{4,6},{5,7},{6,4},{7,5},{8,10},{9,11},{10,... | collective-permute-start | bytes 1179656 | tf_op jit(solution)/shard_map/cond/branch_0_fun/ppermute | solution.py:79
  32.2 0.3 collective-permute-start.6
  33.3 0.1 pad_maximum_fusion.corr_ref
  33.4 3.0 %hidden_0.3 = (bf16[256,768]{1,0:T(8,128)(2,1)S(1)}, f32[1024,768]{1,0:T(8,128)S(1)}, f32[1024,768]{1,0:T(8,128)S(1)}, bf16[1024,1024]{1,0:T(8,128)(2,1)S(1)}, bf16[1024,768]{1,0:T(8,128)(2,1)S(1)}) custom-call(s32[1]{0:T(128)} %bitcast.me_ref, f32[3]{0:T(128)S(1)} %pad_maximum_fusion.corr_ref, bf16[1024,768]{1,0:T(8,128)(2,1)S(1)} %get-tuple-element.91.normed_ref, ...), custom_call_target="tpu_custom_call" | custom-call | flops 1 | bytes 1 | tf_op jit(solution)/shard_map/cond/branch_0_fun/hidden_0/pallas_call | solution.py:408
  36.4 1.3 collective-permute-start.9
  37.6 2.9 %hidden_256.3 = (bf16[256,768]{1,0:T(8,128)(2,1)S(1)}, f32[1024,768]{1,0:T(8,128)S(1)}, f32[1024,768]{1,0:T(8,128)S(1)}, bf16[1024,1024]{1,0:T(8,128)(2,1)S(1)}) custom-call(s32[1]{0:T(128)} %bitcast.me_ref, f32[3]{0:T(128)S(1)} %pad_maximum_fusion.corr_ref, ...), custom_call_target="tpu_custom_call", output_to_operand_aliasing={{1}: (11, {}), {2}: (12, {}), {3}: (13, {})} | custom-call | flops 1 | bytes 1 | tf_op jit(solution)/shard_map/cond/branch_0_fun/hidden_256/pallas_call | solution.py:408
  40.5 0.9 collective-permute-done.7.refs_2_.refs_12_
  41.5 0.8 collective-permute-start.8
  42.2 4.5 %expand_0.3 = (bf16[192,512]{1,0:T(8,128)(2,1)S(1)}, bf16[192,512]{1,0:T(8,128)(2,1)S(1)}, bf16[192,512]{1,0:T(8,128)(2,1)S(1)}, bf16[192,512]{1,0:T(8,128)(2,1)S(1)}, bf16[1024,512]{1,0:T(8,128)(2,1)S(1)}) custom-call(s32[1]{0:T(128)} %bitcast.me_ref, f32[3]{0:T(128)S(1)} %pad_maximum_fusion.corr_ref, bf16[768,1024]{1,0:T(8,128)(2,1)S(1)} %get-tuple-element.90.turned_ref, ...), custom_call_target="tpu_custom_call" | custom-call | flops 1 | bytes 1 | tf_op jit(solution)/shard_map/cond/branch_0_fun/expand_0/pallas_call | solution.py:472
  46.8 0.1 collective-permute-done.9.refs_0_.refs_1_
  46.9 5.5 %hidden_512.3 = (bf16[256,768]{1,0:T(8,128)(2,1)S(1)}, bf16[256,768]{1,0:T(8,128)(2,1)S(1)}, f32[1024,768]{1,0:T(8,128)S(1)}, f32[1024,768]{1,0:T(8,128)S(1)}, bf16[1024,1024]{1,0:T(8,128)(2,1)S(1)}) custom-call(s32[1]{0:T(128)} %bitcast.me_ref, f32[3]{0:T(128)S(1)} %pad_maximum_fusion.corr_ref, ...), custom_call_target="tpu_custom_call", output_to_operand_aliasing={{2}: (11, {}), {3}: (12, {}), {4}: (13, {})} | custom-call | flops 1 | bytes 1 | tf_op jit(solution)/shard_map/cond/branch_0_fun/hidden_512/pallas_call | solution.py:408
  52.5 1.4 collective-permute-start.17
  53.9 1.6 %collective-permute-start.11 = (bf16[192,512]{1,0:T(8,128)(2,1)S(1)}, bf16[192,512]{1,0:T(8,128)(2,1)S(1)}, u32[]{:S(2)}, u32[]{:S(2)}) collective-permute-start(bf16[192,512]{1,0:T(8,128)(2,1)S(1)} %get-tuple-element.111), channel_id=1, source_target_pairs={{0,3},{1,2},{2,1},{3,0},{4,7},{5,6},{6,5},{7,4},{8,11},{9,10},{10,... | collective-permute-start | bytes 589832 | tf_op jit(solution)/shard_map/cond/branch_0_fun/ppermute | solution.py:79
  55.6 0.0 collective-permute-start.15
  55.6 0.9 collective-permute-start.16
  56.5 4.5 %collective-permute-done.11.refs_1_.refs_3_ = bf16[192,512]{1,0:T(8,128)(2,1)S(1)} collective-permute-done((bf16[192,512]{1,0:T(8,128)(2,1)S(1)}, bf16[192,512]{1,0:T(8,128)(2,1)S(1)}, u32[]{:S(2)}, u32[]{:S(2)}) %collective-permute-start.11) | collective-permute-done | bytes 196640 | tf_op jit(solution)/shard_map/cond/branch_0_fun/ppermute | solution.py:79
  61.0 4.3 %collective-permute-done.16.refs_2_ = bf16[192,512]{1,0:T(8,128)(2,1)S(1)} collective-permute-done((bf16[192,512]{1,0:T(8,128)(2,1)S(1)}, bf16[192,512]{1,0:T(8,128)(2,1)S(1)}, u32[]{:S(2)}, u32[]{:S(2)}) %collective-permute-start.16) | collective-permute-done | bytes 196640 | tf_op jit(solution)/shard_map/cond/branch_0_fun/ppermute | solution.py:79
  65.4 5.3 %update_0.3 = (bf16[4,192,512]{2,1,0:T(8,128)(2,1)S(1)}, f32[192,4096]{1,0:T(8,128)}, f32[192,4096]{1,0:T(8,128)}) custom-call(s32[1]{0:T(128)} %bitcast.me_ref, f32[3]{0:T(128)S(1)} %pad_maximum_fusion.corr_ref, bf16[192,4096]{1,0:T(8,128)(2,1)S(1)} %bitcast.64, f32[192,4096]{1,0:T(8,128)S(1)} %bitcast.136, f32[192,4096]{1,0:T(8,128)} %bitcast.142, ...), custom_call_target="tpu_custom_call" | custom-call | flops 1 | bytes 1 | tf_op jit(solution)/shard_map/cond/branch_0_fun/update_0/pallas_call | solution.py:533
  70.6 0.2 collective-permute-start.21
  70.8 1.3 collective-permute-start.10
  72.2 0.1 collective-permute-start.18
  72.3 25.7 %collective-permute-done.10.refs_0_.refs_3_ = bf16[256,768]{1,0:T(8,128)(2,1)S(1)} collective-permute-done((bf16[256,768]{1,0:T(8,128)(2,1)S(1)}, bf16[256,768]{1,0:T(8,128)(2,1)S(1)}, u32[]{:S(2)}, u32[]{:S(2)}) %collective-permute-start.10) | collective-permute-done | bytes 393248 | tf_op jit(solution)/shard_map/cond/branch_0_fun/ppermute | solution.py:118
  98.0 4.6 %expand_512.3 = (bf16[192,512]{1,0:T(8,128)(2,1)S(1)}, bf16[192,512]{1,0:T(8,128)(2,1)S(1)}, bf16[192,512]{1,0:T(8,128)(2,1)S(1)}, bf16[192,512]{1,0:T(8,128)(2,1)S(1)}, bf16[1024,512]{1,0:T(8,128)(2,1)S(1)}) custom-call(s32[1]{0:T(128)} %bitcast.me_ref, f32[3]{0:T(128)S(1)} %pad_maximum_fusion.corr_ref, bf16[768,1024]{1,0:T(8,128)(2,1)S(1)} %get-tuple-element.90.turned_ref, ...), custom_call_target="tpu_custom_call" | custom-call | flops 1 | bytes 1 | tf_op jit(solution)/shard_map/cond/branch_0_fun/expand_512/pallas_call | solution.py:472
  102.5 1.9 %collective-permute-start.12 = (bf16[192,512]{1,0:T(8,128)(2,1)S(1)}, bf16[192,512]{1,0:T(8,128)(2,1)S(1)}, u32[]{:S(2)}, u32[]{:S(2)}) collective-permute-start(bf16[192,512]{1,0:T(8,128)(2,1)S(1)} %get-tuple-element.113), channel_id=1, source_target_pairs={{0,1},{1,0},{2,3},{3,2},{4,5},{5,4},{6,7},{7,6},{8,9},{9,8},{10,11... | collective-permute-start | bytes 589832 | tf_op jit(solution)/shard_map/cond/branch_0_fun/ppermute | solution.py:79
  104.4 1.5 collective-permute-start.13
  105.9 0.2 collective-permute-start.14
  106.1 3.0 %row_grads.3 = (bf16[256,768]{1,0:T(8,128)(2,1)S(1)}, bf16[256,768]{1,0:T(8,128)(2,1)S(1)}, bf16[256,768]{1,0:T(8,128)(2,1)S(1)}, bf16[256,768]{1,0:T(8,128)(2,1)S(1)}) custom-call(s32[1]{0:T(128)} %bitcast.me_ref, bf16[1024,512]{1,0:T(8,128)(2,1)S(1)} %get-tuple-element.109.refs_9_.refs_0_, bf16[1024,512]{1,0:T(8,128)(2,1)S(1)} %get-tuple-element.123.refs_1_, ...), custom_call_target="tpu_custom_call" | custom-call | flops 1 | bytes 1 | tf_op jit(solution)/shard_map/cond/branch_0_fun/row_grads/pallas_call | solution.py:655
  109.1 1.8 %collective-permute-done.13.refs_2_ = bf16[192,512]{1,0:T(8,128)(2,1)S(1)} collective-permute-done((bf16[192,512]{1,0:T(8,128)(2,1)S(1)}, bf16[192,512]{1,0:T(8,128)(2,1)S(1)}, u32[]{:S(2)}, u32[]{:S(2)}) %collective-permute-start.13) | collective-permute-done | bytes 196640 | tf_op jit(solution)/shard_map/cond/branch_0_fun/ppermute | solution.py:79
  110.9 4.4 %collective-permute-done.14.refs_3_ = bf16[192,512]{1,0:T(8,128)(2,1)S(1)} collective-permute-done((bf16[192,512]{1,0:T(8,128)(2,1)S(1)}, bf16[192,512]{1,0:T(8,128)(2,1)S(1)}, u32[]{:S(2)}, u32[]{:S(2)}) %collective-permute-start.14) | collective-permute-done | bytes 196640 | tf_op jit(solution)/shard_map/cond/branch_0_fun/ppermute | solution.py:79
  115.3 3.0 %update_512.3 = (bf16[2,192,512]{2,1,0:T(8,128)(2,1)S(1)}, bf16[2,192,512]{2,1,0:T(8,128)(2,1)S(1)}, f32[192,4096]{1,0:T(8,128)S(1)}, f32[192,4096]{1,0:T(8,128)S(1)}) custom-call(s32[1]{0:T(128)} %bitcast.me_ref, f32[3]{0:T(128)S(1)} %pad_maximum_fusion.corr_ref, bf16[192,4096]{1,0:T(8,128)(2,1)S(1)} %bitcast.65, ...), custom_call_target="tpu_custom_call", output_to_operand_aliasing={{2}: (9, {}), {3}: (10, {})} | custom-call | flops 1 | bytes 1 | tf_op jit(solution)/shard_map/cond/branch_0_fun/update_512/pallas_call | solution.py:533
  118.4 0.0 copy-start.31
  118.4 0.3 collective-permute-start.22
  118.7 1.5 collective-permute-start.23
  120.2 0.4 collective-permute-start.24
  120.6 0.3 collective-permute-start.20
  120.9 1.1 collective-permute-start.19
  122.1 0.6 mean_project.3.refs_4_
  122.6 1.8 %mean_expand_0_0.3.refs_5_.refs_0_ = bf16[192,4096]{1,0:T(8,128)(2,1)} custom-call(s32[1]{0:T(128)} %bitcast.me_ref, bf16[4,192,512]{2,1,0:T(8,128)(2,1)S(1)} %get-tuple-element.124.refs_14_.own_ref, bf16[4,192,512]{2,1,0:T(8,128)(2,1)S(1)} %collective-permute-done.21.other_ref), custom_call_target="tpu_custom_call" | custom-call | flops 1 | bytes 1 | tf_op jit(solution)/shard_map/cond/branch_0_fun/mean_expand_0_0/pallas_call | solution.py:605
  124.5 4.7 %collective-permute-done.23.refs_2_ = bf16[256,768]{1,0:T(8,128)(2,1)S(1)} collective-permute-done((bf16[256,768]{1,0:T(8,128)(2,1)S(1)}, bf16[256,768]{1,0:T(8,128)(2,1)S(1)}, u32[]{:S(2)}, u32[]{:S(2)}) %collective-permute-start.23) | collective-permute-done | bytes 393248 | tf_op jit(solution)/shard_map/cond/branch_0_fun/ppermute | solution.py:79
  129.2 9.1 %collective-permute-done.24.refs_3_ = bf16[256,768]{1,0:T(8,128)(2,1)S(1)} collective-permute-done((bf16[256,768]{1,0:T(8,128)(2,1)S(1)}, bf16[256,768]{1,0:T(8,128)(2,1)S(1)}, u32[]{:S(2)}, u32[]{:S(2)}) %collective-permute-start.24) | collective-permute-done | bytes 393248 | tf_op jit(solution)/shard_map/cond/branch_0_fun/ppermute | solution.py:79
  138.3 1.2 norm_back.3
  139.5 2.9 %collective-permute-start.25 = (bf16[2,8,768]{2,1,0:T(8,128)(2,1)S(1)}, bf16[2,8,768]{2,1,0:T(8,128)(2,1)S(1)}, u32[]{:S(2)}, u32[]{:S(2)}) collective-permute-start(bf16[2,8,768]{2,1,0:T(8,128)(2,1)S(1)} %get-tuple-element.137), channel_id=1, source_target_pairs={{0,1},{1,2},{2,3},{4,5},{5,6},{6,7},{8,9},{9,10},{10,11},{12,13},{... | collective-permute-start | bytes 73736 | tf_op jit(solution)/shard_map/cond/branch_0_fun/ppermute | solution.py:892
  142.5 1.9 %collective-permute-start.26 = (bf16[2,8,768]{2,1,0:T(8,128)(2,1)S(1)}, bf16[2,8,768]{2,1,0:T(8,128)(2,1)S(1)}, u32[]{:S(2)}, u32[]{:S(2)}) collective-permute-start(bf16[2,8,768]{2,1,0:T(8,128)(2,1)S(1)} %get-tuple-element.138), channel_id=1, source_target_pairs={{1,0},{2,1},{3,2},{5,4},{6,5},{7,6},{9,8},{10,9},{11,10},{13,12},{... | collective-permute-start | bytes 73736 | tf_op jit(solution)/shard_map/cond/branch_0_fun/ppermute | solution.py:893
  144.4 3.2 %collective-permute-done.26.high_ref = bf16[2,8,768]{2,1,0:T(8,128)(2,1)S(1)} collective-permute-done((bf16[2,8,768]{2,1,0:T(8,128)(2,1)S(1)}, bf16[2,8,768]{2,1,0:T(8,128)(2,1)S(1)}, u32[]{:S(2)}, u32[]{:S(2)}) %collective-permute-start.26) | collective-permute-done | bytes 24608 | tf_op jit(solution)/shard_map/cond/branch_0_fun/ppermute | solution.py:893
  147.6 1.2 conv_back.3.refs_1_
  148.8 0.9 mean_expand_512_0.3.refs_0_
  149.7 0.8 mean_expand_512_2.3
  (48 shorter events, 0.1 us)
Async XLA Ops:
  1.3 11.2 %collective-permute-start.1 = (bf16[2,128,768]{2,1,0:T(8,128)(2,1)}, bf16[2,128,768]{2,1,0:T(8,128)(2,1)S(1)}, u32[]{:S(2)}, u32[]{:S(2)}) collective-permute-start(bf16[2,128,768]{2,1,0:T(8,128)(2,1)} %bitcast.163), channel_id=1, source_target_pairs={{0,2},{1,3},{2,0},{3,1},{4,6},{5,7},{6,4},{7,5},{8,10},{9,11},{10,... | collective-permute-start | bytes 1179656 | tf_op jit(solution)/shard_map/cond/branch_0_fun/ppermute | solution.py:79
  5.0 2.1 %copy-start.42 = (bf16[1,2,128,768]{3,2,1,0:T(8,128)(2,1)S(1)}, bf16[1,2,128,768]{3,2,1,0:T(8,128)(2,1)}, u32[]{:S(2)}) copy-start(bf16[1,2,128,768]{3,2,1,0:T(8,128)(2,1)} %get-tuple-element.84) | copy-start | bytes 1179652 | tf_op jit(solution)/shard_map/cond
  5.0 9.6 %copy-start.48 = (f32[768]{0:T(1024)S(1)}, f32[768]{0:T(1024)}, u32[]{:S(2)}) copy-start(f32[768]{0:T(1024)} %get-tuple-element.83) | copy-start | bytes 9220 | tf_op jit(solution)/shard_map/cond
  5.0 10.9 %copy-start.45 = (f32[7,768]{1,0:T(8,128)S(1)}, f32[7,768]{1,0:T(8,128)}, u32[]{:S(2)}) copy-start(f32[7,768]{1,0:T(8,128)} %get-tuple-element.82.taps_ref) | copy-start | bytes 64516 | tf_op jit(solution)/shard_map/cond
  5.0 25.6 %copy-start = (bf16[1,192,4096]{2,1,0:T(8,128)(2,1)S(1)}, bf16[1,192,4096]{2,1,0:T(8,128)(2,1)}, u32[]{:S(2)}) copy-start(bf16[1,192,4096]{2,1,0:T(8,128)(2,1)} %get-tuple-element.79) | copy-start | bytes 4718596 | tf_op jit(solution)/shard_map/cond
  6.9 22.4 %collective-permute-start.4 = (bf16[1536,256]{1,0:T(8,128)(2,1)S(1)}, bf16[1536,256]{1,0:T(8,128)(2,1)S(1)}, u32[]{:S(2)}, u32[]{:S(2)}) collective-permute-start(bf16[1536,256]{1,0:T(8,128)(2,1)S(1)} %get-tuple-element.95), channel_id=1, source_target_pairs={{0,2},{1,3},{2,0},{3,1},{4,6},{5,7},{6,4},{7,5},{8,10},{9,11},{10,... | collective-permute-start | bytes 2359304 | tf_op jit(solution)/shard_map/cond/branch_0_fun/ppermute | solution.py:79
  7.0 7.5 %collective-permute-start = (bf16[2,128,768]{2,1,0:T(8,128)(2,1)S(1)}, bf16[2,128,768]{2,1,0:T(8,128)(2,1)S(1)}, u32[]{:S(2)}, u32[]{:S(2)}) collective-permute-start(bf16[2,128,768]{2,1,0:T(8,128)(2,1)S(1)} %bitcast.164), channel_id=1, source_target_pairs={{0,1},{1,0},{2,3},{3,2},{4,5},{5,4},{6,7},{7,6},{8,9},{9,8},{10,11... | collective-permute-start | bytes 1179656 | tf_op jit(solution)/shard_map/cond/branch_0_fun/ppermute | solution.py:79
  12.5 3.4 %collective-permute-start.2 = (bf16[2,128,768]{2,1,0:T(8,128)(2,1)S(1)}, bf16[2,128,768]{2,1,0:T(8,128)(2,1)S(1)}, u32[]{:S(2)}, u32[]{:S(2)}) collective-permute-start(bf16[2,128,768]{2,1,0:T(8,128)(2,1)S(1)} %collective-permute-done.1.refs_2_), channel_id=1, source_target_pairs={{0,1},{1,0},{2,3},{3,2},{4,5},{5,4},{6,7},{7,6},{8,9},{9,8},{10,11... | collective-permute-start | bytes 1179656 | tf_op jit(solution)/shard_map/cond/branch_0_fun/ppermute | solution.py:79
  14.6 18.8 %collective-permute-start.3 = (bf16[1536,256]{1,0:T(8,128)(2,1)S(1)}, bf16[1536,256]{1,0:T(8,128)(2,1)S(1)}, u32[]{:S(2)}, u32[]{:S(2)}) collective-permute-start(bf16[1536,256]{1,0:T(8,128)(2,1)S(1)} %get-tuple-element.88.refs_0_.refs_4_.refs_2_.refs_6_), channel_id=1, source_target_pairs={{0,1},{1,0},{2,3},{3,2},{4,5},{5,4},{6,7},{7,6},{8,9},{9,8},{10,11... | collective-permute-start | bytes 2359304 | tf_op jit(solution)/shard_map/cond/branch_0_fun/ppermute | solution.py:79
  15.9 17.5 %copy-start.9 = (f32[1,1024,768]{2,1,0:T(8,128)S(1)}, f32[1,1024,768]{2,1,0:T(8,128)}, u32[]{:S(2)}) copy-start(f32[1,1024,768]{2,1,0:T(8,128)} %get-tuple-element.94) | copy-start | bytes 9437188 | tf_op jit(solution)/shard_map/cond
  29.3 4.0 %copy-start.3 = (bf16[1,1024,768]{2,1,0:T(8,128)(2,1)S(1)}, bf16[1,1024,768]{2,1,0:T(8,128)(2,1)}, u32[]{:S(2)}) copy-start(bf16[1,1024,768]{2,1,0:T(8,128)(2,1)} %get-tuple-element.92) | copy-start | bytes 4718596 | tf_op jit(solution)/shard_map/cond
  29.4 4.0 %copy-start.6 = (f32[1,1024,768]{2,1,0:T(8,128)S(1)}, f32[1,1024,768]{2,1,0:T(8,128)}, u32[]{:S(2)}) copy-start(f32[1,1024,768]{2,1,0:T(8,128)} %get-tuple-element.93) | copy-start | bytes 9437188 | tf_op jit(solution)/shard_map/cond
  29.4 4.0 %collective-permute-start.5 = (bf16[1536,256]{1,0:T(8,128)(2,1)S(1)}, bf16[1536,256]{1,0:T(8,128)(2,1)S(1)}, u32[]{:S(2)}, u32[]{:S(2)}) collective-permute-start(bf16[1536,256]{1,0:T(8,128)(2,1)S(1)} %collective-permute-done.4.refs_2_.refs_6_.refs_4_.refs_8_), channel_id=1, source_target_pairs={{0,1},{1,0},{2,3},{3,2},{4,5},{5,4},{6,7},{7,6},{8,9},{9,8},{10,11... | collective-permute-start | bytes 2359304 | tf_op jit(solution)/shard_map/cond/branch_0_fun/ppermute | solution.py:79
  30.6 10.8 %collective-permute-start.7 = (bf16[384,512]{1,0:T(8,128)(2,1)S(1)}, bf16[384,512]{1,0:T(8,128)(2,1)S(1)}, u32[]{:S(2)}, u32[]{:S(2)}) collective-permute-start(bf16[384,512]{1,0:T(8,128)(2,1)S(1)} %get-tuple-element.99), channel_id=1, source_target_pairs={{0,2},{1,3},{2,0},{3,1},{4,6},{5,7},{6,4},{7,5},{8,10},{9,11},{10,... | collective-permute-start | bytes 1179656 | tf_op jit(solution)/shard_map/cond/branch_0_fun/ppermute | solution.py:79
  32.2 14.8 %collective-permute-start.6 = (bf16[384,512]{1,0:T(8,128)(2,1)S(1)}, bf16[384,512]{1,0:T(8,128)(2,1)S(1)}, u32[]{:S(2)}, u32[]{:S(2)}) collective-permute-start(bf16[384,512]{1,0:T(8,128)(2,1)S(1)} %get-tuple-element.98.refs_0_.refs_10_), channel_id=1, source_target_pairs={{0,1},{1,0},{2,3},{3,2},{4,5},{5,4},{6,7},{7,6},{8,9},{9,8},{10,11... | collective-permute-start | bytes 1179656 | tf_op jit(solution)/shard_map/cond/branch_0_fun/ppermute | solution.py:79
  36.4 10.6 %collective-permute-start.9 = (bf16[256,768]{1,0:T(8,128)(2,1)S(1)}, bf16[256,768]{1,0:T(8,128)(2,1)S(1)}, u32[]{:S(2)}, u32[]{:S(2)}) collective-permute-start(bf16[256,768]{1,0:T(8,128)(2,1)S(1)} %get-tuple-element.108.refs_0_), channel_id=1, source_target_pairs={{0,4},{4,0},{8,12},{12,8},{16,20},{20,16},{24,28},{28,24},{1,5},{5... | collective-permute-start | bytes 1179656 | tf_op jit(solution)/shard_map/cond/branch_0_fun/ppermute | solution.py:118
  41.5 5.5 %collective-permute-start.8 = (bf16[384,512]{1,0:T(8,128)(2,1)S(1)}, bf16[384,512]{1,0:T(8,128)(2,1)S(1)}, u32[]{:S(2)}, u32[]{:S(2)}) collective-permute-start(bf16[384,512]{1,0:T(8,128)(2,1)S(1)} %collective-permute-done.7.refs_2_.refs_12_), channel_id=1, source_target_pairs={{0,1},{1,0},{2,3},{3,2},{4,5},{5,4},{6,7},{7,6},{8,9},{9,8},{10,11... | collective-permute-start | bytes 1179656 | tf_op jit(solution)/shard_map/cond/branch_0_fun/ppermute | solution.py:79
  46.9 18.4 %copy-start.18 = (f32[1,192,4096]{2,1,0:T(8,128)S(1)}, f32[1,192,4096]{2,1,0:T(8,128)}, u32[]{:S(2)}) copy-start(f32[1,192,4096]{2,1,0:T(8,128)} %get-tuple-element.80) | copy-start | bytes 9437188 | tf_op jit(solution)/shard_map/cond
  52.5 18.1 %copy-start.12 = (f32[1024,768]{1,0:T(8,128)}, f32[1024,768]{1,0:T(8,128)S(1)}, u32[]{:S(2)}) copy-start(f32[1024,768]{1,0:T(8,128)S(1)} %get-tuple-element.142) | copy-start | bytes 9437188 | tf_op jit(solution)/shard_map/cond
  52.5 18.1 %copy-start.15 = (f32[1024,768]{1,0:T(8,128)}, f32[1024,768]{1,0:T(8,128)S(1)}, u32[]{:S(2)}) copy-start(f32[1024,768]{1,0:T(8,128)S(1)} %get-tuple-element.143) | copy-start | bytes 9437188 | tf_op jit(solution)/shard_map/cond
  52.5 12.8 %collective-permute-start.17 = (bf16[256,768]{1,0:T(8,128)(2,1)S(1)}, bf16[256,768]{1,0:T(8,128)(2,1)S(1)}, u32[]{:S(2)}, u32[]{:S(2)}) collective-permute-start(bf16[256,768]{1,0:T(8,128)(2,1)S(1)} %get-tuple-element.119.refs_4_), channel_id=1, source_target_pairs={{0,4},{4,0},{8,12},{12,8},{16,20},{20,16},{24,28},{28,24},{1,5},{5... | collective-permute-start | bytes 1179656 | tf_op jit(solution)/shard_map/cond/branch_0_fun/ppermute | solution.py:118
  53.9 7.1 %collective-permute-start.11 = (bf16[192,512]{1,0:T(8,128)(2,1)S(1)}, bf16[192,512]{1,0:T(8,128)(2,1)S(1)}, u32[]{:S(2)}, u32[]{:S(2)}) collective-permute-start(bf16[192,512]{1,0:T(8,128)(2,1)S(1)} %get-tuple-element.111), channel_id=1, source_target_pairs={{0,3},{1,2},{2,1},{3,0},{4,7},{5,6},{6,5},{7,4},{8,11},{9,10},{10,... | collective-permute-start | bytes 589832 | tf_op jit(solution)/shard_map/cond/branch_0_fun/ppermute | solution.py:79
  55.6 5.4 %collective-permute-start.15 = (bf16[192,512]{1,0:T(8,128)(2,1)S(1)}, bf16[192,512]{1,0:T(8,128)(2,1)S(1)}, u32[]{:S(2)}, u32[]{:S(2)}) collective-permute-start(bf16[192,512]{1,0:T(8,128)(2,1)S(1)} %get-tuple-element.117), channel_id=1, source_target_pairs={{0,1},{1,0},{2,3},{3,2},{4,5},{5,4},{6,7},{7,6},{8,9},{9,8},{10,11... | collective-permute-start | bytes 589832 | tf_op jit(solution)/shard_map/cond/branch_0_fun/ppermute | solution.py:79
  55.6 9.8 %collective-permute-start.16 = (bf16[192,512]{1,0:T(8,128)(2,1)S(1)}, bf16[192,512]{1,0:T(8,128)(2,1)S(1)}, u32[]{:S(2)}, u32[]{:S(2)}) collective-permute-start(bf16[192,512]{1,0:T(8,128)(2,1)S(1)} %get-tuple-element.118), channel_id=1, source_target_pairs={{0,2},{1,3},{2,0},{3,1},{4,6},{5,7},{6,4},{7,5},{8,10},{9,11},{10,... | collective-permute-start | bytes 589832 | tf_op jit(solution)/shard_map/cond/branch_0_fun/ppermute | solution.py:79
  70.6 50.3 %collective-permute-start.21 = (bf16[4,192,512]{2,1,0:T(8,128)(2,1)S(1)}, bf16[4,192,512]{2,1,0:T(8,128)(2,1)S(1)}, u32[]{:S(2)}, u32[]{:S(2)}) collective-permute-start(bf16[4,192,512]{2,1,0:T(8,128)(2,1)S(1)} %get-tuple-element.124.refs_14_.own_ref), channel_id=1, source_target_pairs={{0,4},{4,0},{8,12},{12,8},{16,20},{20,16},{24,28},{28,24},{1,5},{5... | collective-permute-start | bytes 2359304 | tf_op jit(solution)/shard_map/cond/branch_0_fun/ppermute | solution.py:118
  70.8 27.1 %collective-permute-start.10 = (bf16[256,768]{1,0:T(8,128)(2,1)S(1)}, bf16[256,768]{1,0:T(8,128)(2,1)S(1)}, u32[]{:S(2)}, u32[]{:S(2)}) collective-permute-start(bf16[256,768]{1,0:T(8,128)(2,1)S(1)} %get-tuple-element.103.refs_2_), channel_id=1, source_target_pairs={{0,4},{4,0},{8,12},{12,8},{16,20},{20,16},{24,28},{28,24},{1,5},{5... | collective-permute-start | bytes 1179656 | tf_op jit(solution)/shard_map/cond/branch_0_fun/ppermute | solution.py:118
  72.2 43.1 %collective-permute-start.18 = (bf16[256,768]{1,0:T(8,128)(2,1)S(1)}, bf16[256,768]{1,0:T(8,128)(2,1)S(1)}, u32[]{:S(2)}, u32[]{:S(2)}) collective-permute-start(bf16[256,768]{1,0:T(8,128)(2,1)S(1)} %get-tuple-element.122.refs_6_), channel_id=1, source_target_pairs={{0,4},{4,0},{8,12},{12,8},{16,20},{20,16},{24,28},{28,24},{1,5},{5... | collective-permute-start | bytes 1179656 | tf_op jit(solution)/shard_map/cond/branch_0_fun/ppermute | solution.py:118
  102.5 6.6 %collective-permute-start.12 = (bf16[192,512]{1,0:T(8,128)(2,1)S(1)}, bf16[192,512]{1,0:T(8,128)(2,1)S(1)}, u32[]{:S(2)}, u32[]{:S(2)}) collective-permute-start(bf16[192,512]{1,0:T(8,128)(2,1)S(1)} %get-tuple-element.113), channel_id=1, source_target_pairs={{0,1},{1,0},{2,3},{3,2},{4,5},{5,4},{6,7},{7,6},{8,9},{9,8},{10,11... | collective-permute-start | bytes 589832 | tf_op jit(solution)/shard_map/cond/branch_0_fun/ppermute | solution.py:79
  104.4 6.5 %collective-permute-start.13 = (bf16[192,512]{1,0:T(8,128)(2,1)S(1)}, bf16[192,512]{1,0:T(8,128)(2,1)S(1)}, u32[]{:S(2)}, u32[]{:S(2)}) collective-permute-start(bf16[192,512]{1,0:T(8,128)(2,1)S(1)} %get-tuple-element.114), channel_id=1, source_target_pairs={{0,2},{1,3},{2,0},{3,1},{4,6},{5,7},{6,4},{7,5},{8,10},{9,11},{10,... | collective-permute-start | bytes 589832 | tf_op jit(solution)/shard_map/cond/branch_0_fun/ppermute | solution.py:79
  105.9 9.4 %collective-permute-start.14 = (bf16[192,512]{1,0:T(8,128)(2,1)S(1)}, bf16[192,512]{1,0:T(8,128)(2,1)S(1)}, u32[]{:S(2)}, u32[]{:S(2)}) collective-permute-start(bf16[192,512]{1,0:T(8,128)(2,1)S(1)} %get-tuple-element.115), channel_id=1, source_target_pairs={{0,3},{1,2},{2,1},{3,0},{4,7},{5,6},{6,5},{7,4},{8,11},{9,10},{10,... | collective-permute-start | bytes 589832 | tf_op jit(solution)/shard_map/cond/branch_0_fun/ppermute | solution.py:79
  106.1 9.2 %copy-start.21 = (f32[1,192,4096]{2,1,0:T(8,128)S(1)}, f32[1,192,4096]{2,1,0:T(8,128)}, u32[]{:S(2)}) copy-start(f32[1,192,4096]{2,1,0:T(8,128)} %get-tuple-element.81) | copy-start | bytes 9437188 | tf_op jit(solution)/shard_map/cond
  106.1 9.2 %copy-start.24 = (f32[192,4096]{1,0:T(8,128)S(1)}, f32[192,4096]{1,0:T(8,128)}, u32[]{:S(2)}) copy-start(f32[192,4096]{1,0:T(8,128)} %get-tuple-element.120.refs_4_) | copy-start | bytes 9437188 | tf_op jit(solution)/shard_map/cond
  106.1 9.2 %copy-start.30 = (f32[192,4096]{1,0:T(8,128)S(1)}, f32[192,4096]{1,0:T(8,128)}, u32[]{:S(2)}) copy-start(f32[192,4096]{1,0:T(8,128)} %get-tuple-element.121.refs_5_) | copy-start | bytes 9437188 | tf_op jit(solution)/shard_map/cond
  118.4 6.1 %copy-start.25 = (f32[192,4096]{1,0:T(8,128)}, f32[192,4096]{1,0:T(8,128)S(1)}, u32[]{:S(2)}) copy-start(f32[192,4096]{1,0:T(8,128)S(1)} %get-tuple-element.140) | copy-start | bytes 9437188 | tf_op jit(solution)/shard_map/cond
  118.4 6.1 %copy-start.31 = (f32[192,4096]{1,0:T(8,128)}, f32[192,4096]{1,0:T(8,128)S(1)}, u32[]{:S(2)}) copy-start(f32[192,4096]{1,0:T(8,128)S(1)} %get-tuple-element.141) | copy-start | bytes 9437188 | tf_op jit(solution)/shard_map/cond
  118.4 6.1 %collective-permute-start.22 = (bf16[256,768]{1,0:T(8,128)(2,1)S(1)}, bf16[256,768]{1,0:T(8,128)(2,1)S(1)}, u32[]{:S(2)}, u32[]{:S(2)}) collective-permute-start(bf16[256,768]{1,0:T(8,128)(2,1)S(1)} %get-tuple-element.131), channel_id=1, source_target_pairs={{0,1},{1,0},{2,3},{3,2},{4,5},{5,4},{6,7},{7,6},{8,9},{9,8},{10,11... | collective-permute-start | bytes 1179656 | tf_op jit(solution)/shard_map/cond/branch_0_fun/ppermute | solution.py:79
  118.7 10.5 %collective-permute-start.23 = (bf16[256,768]{1,0:T(8,128)(2,1)S(1)}, bf16[256,768]{1,0:T(8,128)(2,1)S(1)}, u32[]{:S(2)}, u32[]{:S(2)}) collective-permute-start(bf16[256,768]{1,0:T(8,128)(2,1)S(1)} %get-tuple-element.134), channel_id=1, source_target_pairs={{0,2},{1,3},{2,0},{3,1},{4,6},{5,7},{6,4},{7,5},{8,10},{9,11},{10,... | collective-permute-start | bytes 1179656 | tf_op jit(solution)/shard_map/cond/branch_0_fun/ppermute | solution.py:79
  120.2 18.1 %collective-permute-start.24 = (bf16[256,768]{1,0:T(8,128)(2,1)S(1)}, bf16[256,768]{1,0:T(8,128)(2,1)S(1)}, u32[]{:S(2)}, u32[]{:S(2)}) collective-permute-start(bf16[256,768]{1,0:T(8,128)(2,1)S(1)} %get-tuple-element.135), channel_id=1, source_target_pairs={{0,3},{1,2},{2,1},{3,0},{4,7},{5,6},{6,5},{7,4},{8,11},{9,10},{10,... | collective-permute-start | bytes 1179656 | tf_op jit(solution)/shard_map/cond/branch_0_fun/ppermute | solution.py:79
  120.6 28.2 %collective-permute-start.20 = (bf16[2,192,512]{2,1,0:T(8,128)(2,1)S(1)}, bf16[2,192,512]{2,1,0:T(8,128)(2,1)S(1)}, u32[]{:S(2)}, u32[]{:S(2)}) collective-permute-start(bf16[2,192,512]{2,1,0:T(8,128)(2,1)S(1)} %get-tuple-element.127.own_ref), channel_id=1, source_target_pairs={{0,4},{4,0},{8,12},{12,8},{16,20},{20,16},{24,28},{28,24},{1,5},{5... | collective-permute-start | bytes 1179656 | tf_op jit(solution)/shard_map/cond/branch_0_fun/ppermute | solution.py:118
  120.9 28.8 %collective-permute-start.19 = (bf16[2,192,512]{2,1,0:T(8,128)(2,1)S(1)}, bf16[2,192,512]{2,1,0:T(8,128)(2,1)S(1)}, u32[]{:S(2)}, u32[]{:S(2)}) collective-permute-start(bf16[2,192,512]{2,1,0:T(8,128)(2,1)S(1)} %get-tuple-element.126.own_ref), channel_id=1, source_target_pairs={{0,4},{4,0},{8,12},{12,8},{16,20},{20,16},{24,28},{28,24},{1,5},{5... | collective-permute-start | bytes 1179656 | tf_op jit(solution)/shard_map/cond/branch_0_fun/ppermute | solution.py:118
  122.6 16.9 %copy-start.36 = (bf16[1024,768]{1,0:T(8,128)(2,1)}, bf16[1024,768]{1,0:T(8,128)(2,1)S(1)}, u32[]{:S(2)}) copy-start(bf16[1024,768]{1,0:T(8,128)(2,1)S(1)} %mean_project.3.refs_4_) | copy-start | bytes 4718596 | tf_op jit(solution)/shard_map/cond
  139.5 4.9 %collective-permute-start.25 = (bf16[2,8,768]{2,1,0:T(8,128)(2,1)S(1)}, bf16[2,8,768]{2,1,0:T(8,128)(2,1)S(1)}, u32[]{:S(2)}, u32[]{:S(2)}) collective-permute-start(bf16[2,8,768]{2,1,0:T(8,128)(2,1)S(1)} %get-tuple-element.137), channel_id=1, source_target_pairs={{0,1},{1,2},{2,3},{4,5},{5,6},{6,7},{8,9},{9,10},{10,11},{12,13},{... | collective-permute-start | bytes 73736 | tf_op jit(solution)/shard_map/cond/branch_0_fun/ppermute | solution.py:892
  142.5 5.1 %collective-permute-start.26 = (bf16[2,8,768]{2,1,0:T(8,128)(2,1)S(1)}, bf16[2,8,768]{2,1,0:T(8,128)(2,1)S(1)}, u32[]{:S(2)}, u32[]{:S(2)}) collective-permute-start(bf16[2,8,768]{2,1,0:T(8,128)(2,1)S(1)} %get-tuple-element.138), channel_id=1, source_target_pairs={{1,0},{2,1},{3,2},{5,4},{6,5},{7,6},{9,8},{10,9},{11,10},{13,12},{... | collective-permute-start | bytes 73736 | tf_op jit(solution)/shard_map/cond/branch_0_fun/ppermute | solution.py:893
  148.8 1.8 %copy-start.39 = (bf16[2,128,768]{2,1,0:T(8,128)(2,1)}, bf16[2,128,768]{2,1,0:T(8,128)(2,1)S(1)}, u32[]{:S(2)}) copy-start(bf16[2,128,768]{2,1,0:T(8,128)(2,1)S(1)} %conv_back.3.refs_1_) | copy-start | bytes 1179652 | tf_op jit(solution)/shard_map/cond
